TPU v7x, 128 devices: a whole 4x4x4 slice. The times are simulated.
128 devices in a mesh: blk: 2 (over x_lo), mblk: 64 (over z, y, x_hi, core).
Axes of the slice: x: 4 (x_hi: 2, x_lo: 2; x = x_hi * 2 + x_lo), y: 4, z: 4, core: 2. Of those that a mesh axis runs over, the one named last changes fastest.
Arguments:
- pixels: float32 [2048, 1024], P(('blk', 'mblk')), may hold values from -6 to 6
- block_ids: int32 [2048], P(('blk', 'mblk')), may hold values from 0 to 2047, as said below
- block_mask: int32 [2048], P(('blk', 'mblk')), may hold values 0 or 1
- model_cl: float32 [4096], replicated, may hold values from 0.5 to 1.5
Outputs:
- pseudo_cl: float32 [4096], replicated
- misfit: float32 [], replicated
Inputs may be any that keep to these rules, and one draw needn't show every extreme that they name: block_ids holds every block number once. The device at blk index s and mblk index j holds, for every blk index b, exactly 8 blocks of the cycles of the device at blk index b and mblk index j, where cycle r belongs to the device at blk index r // 128 and mblk index (r % 128) // 2.
All inputs are finite; a program needn't handle non-finite values. No bound on the sum of `block_mask` on one device may be relied on, other than what follows from the above.
Results may differ from a plain program's by a relative error of at most 0.0003.
Values sent between devices are 32-bit elements; how exact they have to be, the bound alone decides.
A program may use at most 64 MiB of HBM per device.

v0:
```python
import math

import jax
import jax.numpy as jnp
from jax import lax
from jax.sharding import PartitionSpec as P

NSIDE = 2048
CYCLE_PIX = 8192
LMAX = 4096
BLOCK_PIX = 1024
SEGS = 8


def log_products(degree_count):
    counter = jnp.arange(1, degree_count, dtype=jnp.int32).astype(jnp.float32)
    return jnp.concatenate([jnp.zeros((1,), jnp.float32), jnp.cumsum(jnp.log1p(-0.5 / counter))])


def seeds_for(latitude, orders_f, log_prod):
    base_log = 0.5 * (jnp.log(2.0 * orders_f + 1.0) - math.log(4.0 * math.pi)) + 0.5 * log_prod
    return jnp.exp(
        base_log[None, :]
        + 0.5 * orders_f[None, :] * jnp.log1p(-latitude[:, None] * latitude[:, None])
    )


def coefficients(degree_f, orders_f):
    alpha_term = jnp.sqrt(
        (2.0 * degree_f - 1.0)
        * (2.0 * degree_f + 1.0)
        / jnp.maximum((degree_f - orders_f) * (degree_f + orders_f), 1.0)
    )
    beta_term = alpha_term * jnp.sqrt(
        jnp.maximum((degree_f - 1.0 - orders_f) * (degree_f - 1.0 + orders_f), 0.0)
        / jnp.maximum((2.0 * degree_f - 3.0) * (2.0 * degree_f - 1.0), 1.0)
    )
    return (alpha_term, beta_term)


def advance_rows(degree, orders, latitude, prev_one, prev_two, seed_rows):
    degree_f = degree.astype(jnp.float32)
    orders_f = orders.astype(jnp.float32)
    alpha_term, beta_term = coefficients(degree_f, orders_f)
    grown = alpha_term[:, None] * latitude[None, :] * prev_one - beta_term[:, None] * prev_two
    return jnp.where(
        degree > orders[:, None], grown, jnp.where(degree == orders[:, None], seed_rows, 0.0)
    )


def cycle_spectra(cycle_rows, cycle_index):
    cycle_count, cycle_len = cycle_rows.shape
    inner_len = min(128, cycle_len)
    outer_len = cycle_len // inner_len
    kept_orders = cycle_len // 2
    upper_len = kept_orders // outer_len
    highest = lax.Precision.HIGHEST
    folded = cycle_rows.reshape(cycle_count, outer_len, inner_len)
    outer_idx = jnp.arange(outer_len, dtype=jnp.int32)
    inner_idx = jnp.arange(inner_len, dtype=jnp.int32)
    upper_idx = jnp.arange(upper_len, dtype=jnp.int32)
    angle_one = (outer_idx[:, None] * outer_idx[None, :] % outer_len).astype(jnp.float32) * (
        2.0 * math.pi / outer_len
    )
    section_re = jnp.einsum("rap,ak->rkp", folded, jnp.cos(angle_one), precision=highest)
    section_im = -jnp.einsum("rap,ak->rkp", folded, jnp.sin(angle_one), precision=highest)
    twist = (outer_idx[:, None] * inner_idx[None, :] % cycle_len).astype(jnp.float32) * (
        2.0 * math.pi / cycle_len
    )
    twist_cos = jnp.cos(twist)[None]
    twist_sin = jnp.sin(twist)[None]
    turned_re = section_re * twist_cos + section_im * twist_sin
    turned_im = section_im * twist_cos - section_re * twist_sin
    angle_two = (inner_idx[:, None] * upper_idx[None, :] % inner_len).astype(jnp.float32) * (
        2.0 * math.pi / inner_len
    )
    cos_two = jnp.cos(angle_two)
    sin_two = jnp.sin(angle_two)
    out_re = jnp.einsum("rkp,pq->rkq", turned_re, cos_two, precision=highest) + jnp.einsum(
        "rkp,pq->rkq", turned_im, sin_two, precision=highest
    )
    out_im = jnp.einsum("rkp,pq->rkq", turned_im, cos_two, precision=highest) - jnp.einsum(
        "rkp,pq->rkq", turned_re, sin_two, precision=highest
    )
    out_re = jnp.transpose(out_re, (0, 2, 1)).reshape(cycle_count, kept_orders)
    out_im = jnp.transpose(out_im, (0, 2, 1)).reshape(cycle_count, kept_orders)
    orders_f = jnp.arange(kept_orders, dtype=jnp.int32).astype(jnp.float32)
    half_shift = jnp.where(cycle_index % 2 == 0, 0.5, 0.0).astype(jnp.float32)
    phase_angle = half_shift[:, None] * orders_f[None, :] * (2.0 * math.pi / cycle_len)
    phase_cos = jnp.cos(phase_angle)
    phase_sin = jnp.sin(phase_angle)
    spec_re = out_re * phase_cos + out_im * phase_sin
    spec_im = out_im * phase_cos - out_re * phase_sin
    return jnp.stack([spec_re, spec_im])


def recurrence(spectra, latitude, chosen, log_prod, block_len, norm_scale):
    degree_count = log_prod.shape[0]
    group_size = chosen.shape[0]
    spec_rows = jnp.transpose(spectra, (0, 2, 1))
    seed_rows = jnp.transpose(seeds_for(latitude, chosen.astype(jnp.float32), log_prod[chosen]))
    first_block = jnp.min(chosen) // block_len
    zero_state = jnp.zeros((group_size, latitude.shape[0]), jnp.float32)

    def one_block(block_idx, carried):
        prev_one, prev_two, result = carried
        base_degree = block_idx * block_len

        def sixteen_rows(part_idx, inner_state):
            state_one, state_two, buffer = inner_state
            row_list = []
            for offset in range(16):
                degree = base_degree + part_idx * 16 + offset
                fresh_row = advance_rows(degree, chosen, latitude, state_one, state_two, seed_rows)
                state_two = state_one
                state_one = fresh_row
                row_list.append(
                    jnp.stack(
                        [
                            jnp.sum(fresh_row * spec_rows[0], axis=1),
                            jnp.sum(fresh_row * spec_rows[1], axis=1),
                        ]
                    )
                )
            stacked = jnp.stack(row_list, axis=1)
            return (
                state_one,
                state_two,
                lax.dynamic_update_slice_in_dim(buffer, stacked, part_idx * 16, 1),
            )

        empty_buffer = jnp.zeros((2, block_len, group_size), jnp.float32)
        prev_one, prev_two, buffer = lax.fori_loop(
            0, block_len // 16, sixteen_rows, (prev_one, prev_two, empty_buffer)
        )
        placed = jnp.transpose(buffer * norm_scale, (2, 0, 1))
        return (prev_one, prev_two, lax.dynamic_update_slice_in_dim(result, placed, base_degree, 2))

    empty_result = jnp.zeros((group_size, 2, degree_count), jnp.float32)
    return lax.fori_loop(
        first_block, degree_count // block_len, one_block, (zero_state, zero_state, empty_result)
    )[2]


def legendre(band_rows, latitude, orders, log_prod, start_row, row_total, group_size, norm_scale):
    degree_count = log_prod.shape[0]
    block_len = min(256, degree_count)

    def one_group(group_idx, result):
        offset = start_row + group_idx * group_size
        spectra = lax.dynamic_slice_in_dim(band_rows, offset, group_size, 2)
        chosen = lax.dynamic_slice_in_dim(orders, offset, group_size, 0)
        group_rows = recurrence(spectra, latitude, chosen, log_prod, block_len, norm_scale)
        return lax.dynamic_update_slice_in_dim(result, group_rows, group_idx * group_size, 0)

    return lax.fori_loop(
        0, row_total // group_size, one_group, jnp.zeros((row_total, 2, degree_count), jnp.float32)
    )


def arrange(spectra, groups):
    spec_pair, cycle_count, order_count = spectra.shape
    return spectra.reshape(spec_pair, cycle_count, groups, order_count // groups)


def owned_orders(group_idx, groups, order_count):
    per_group = order_count // groups
    return group_idx * per_group + jnp.arange(per_group, dtype=jnp.int32)


def power_part(alm_rows, chosen):
    weights = jnp.where(chosen == 0, 1.0, 2.0).astype(jnp.float32)
    return jnp.sum(
        weights[:, None] * (alm_rows[:, 0] * alm_rows[:, 0] + alm_rows[:, 1] * alm_rows[:, 1]),
        axis=0,
    )


def latitudes(cycle_idx, cycles_all):
    return (cycles_all // 2 - cycle_idx).astype(jnp.float32) * (2.0 / (3.0 * NSIDE))


def on_device(pixels, block_ids, block_mask, model_cl):
    n_blk = lax.axis_size("blk")
    n_mblk = lax.axis_size("mblk")
    blk_idx = lax.axis_index("blk")
    mblk_idx = lax.axis_index("mblk")
    slots = pixels.shape[0]
    cap_band = slots // n_blk
    cycle_dev = slots // SEGS
    r_band = cycle_dev * n_mblk
    cycles_all = r_band * n_blk
    norm_scale = math.sqrt(4.0 * math.pi / (cycles_all * CYCLE_PIX))
    kept_pixels = pixels * block_mask[:, None].astype(jnp.float32)
    band_of = block_ids // SEGS // r_band
    sorting = jnp.argsort(band_of * slots + jnp.arange(slots, dtype=jnp.int32))
    outgoing = kept_pixels[sorting].reshape(n_blk, cap_band, BLOCK_PIX)
    outgoing_ids = block_ids[sorting].reshape(n_blk, cap_band)
    got_blocks, got_ids = (
        lax.all_to_all(outgoing, "blk", split_axis=0, concat_axis=0, tiled=True),
        lax.all_to_all(outgoing_ids, "blk", split_axis=0, concat_axis=0, tiled=True),
    )
    owner = blk_idx * n_mblk + mblk_idx
    slot_pos = got_ids.reshape(-1) - owner * slots
    cycle_rows = (
        jnp.zeros((slots, BLOCK_PIX), jnp.float32)
        .at[slot_pos]
        .set(got_blocks.reshape(slots, BLOCK_PIX))
    )
    cycle_rows = cycle_rows.reshape(cycle_dev, CYCLE_PIX)
    cycle_index = owner * cycle_dev + jnp.arange(cycle_dev, dtype=jnp.int32)
    spectra = cycle_spectra(cycle_rows, cycle_index)
    log_prod = log_products(LMAX)
    sent = arrange(spectra, n_mblk)
    got_rows = lax.all_to_all(sent, "mblk", split_axis=2, concat_axis=1, tiled=True)
    band_rows = got_rows.reshape(2, r_band, -1)
    latitude = latitudes(blk_idx * r_band + jnp.arange(r_band, dtype=jnp.int32), cycles_all)
    orders = owned_orders(mblk_idx, n_mblk, LMAX)
    per_dev = orders.shape[0]
    row_count = per_dev // n_blk
    group_size = math.gcd(row_count, per_dev // 2)
    partial_alm = legendre(
        band_rows, latitude, orders, log_prod, 0, per_dev, group_size, norm_scale
    )
    alm_rows = lax.psum(partial_alm, "blk")
    power_sum = lax.psum(power_part(alm_rows, orders), "mblk")
    degrees_f = jnp.arange(LMAX, dtype=jnp.int32).astype(jnp.float32)
    pseudo_cl = power_sum / (2.0 * degrees_f + 1.0)
    rel_error = (pseudo_cl - model_cl) / model_cl
    misfit = jnp.mean(rel_error * rel_error)
    return (pseudo_cl, misfit)


def solution(mesh):
    in_specs = (P(("blk", "mblk"), None), P(("blk", "mblk")), P(("blk", "mblk")), P())
    out_specs = (P(), P())
    return jax.shard_map(
        on_device, mesh=mesh, in_specs=in_specs, out_specs=out_specs, check_vma=False
    )
```

profile of v0, /device:TPU:1, one launch (start us, length us, event | category | flops | bytes accessed | tf_op | source)
XLA Modules:
  0.0 2473.2 jit_solution(6680545544918671897)
XLA Ops:
  55.7 1970.1 %while.94 = (s32[]{:T(128)}, f32[64,2,4096]{0,1,2:T(2,128)}, s32[64]{0:T(128)S(1)}, f32[4096]{0:T(1024)S(1)}, f32[2,128,64]{1,2,0:T(8,128)S(1)}, /*index=5*/s32[...) while((s32[]{:T(128)}, f32[64,2,4096]{0,1,2:T(2,128)}, ...), condition=%wide.region_42.43_spmd.clone.clone, body=%wide.region_4.42_spmd.clone.clone.sunk | while | flops 689471 | bytes 4468927 | solution.py:156
  62.7 578.5 %while.95 = (s32[]{:T(128)}, f32[32,128]{1,0:T(8,128)S(1)}, f32[32,128]{1,0:T(8,128)S(1)}, f32[32,2,4096]{0,1,2:T(2,128)}, s32[32]{0:T(128)S(1)}, /*index=5*/f32...) while((s32[]{:T(128)}, f32[32,128]{1,0:T(8,128)S(1)}, ...), condition=%wide.region_41.41_spmd.clone, body=%wide.region_6.40_spmd.clone.sunk | while | flops 686763 | bytes 1217226 | solution.py:140
  62.9 35.1 %while.96 = (s32[]{:T(128)}, f32[32,128]{1,0:T(8,128)S(1)}, f32[32,128]{1,0:T(8,128)S(1)}, f32[2,256,32]{2,0,1:T(2,128)S(1)}, s32[]{:T(128)}, /*index=5*/s32[32]...) while((s32[]{:T(128)}, f32[32,128]{1,0:T(8,128)S(1)}, ...), condition=%wide.region_40.39_spmd, body=%wide.region_7.38_spmd.sunk | while | flops 662181 | bytes 806215 | solution.py:133
  99.0 35.1 %while.96 = (s32[]{:T(128)}, f32[32,128]{1,0:T(8,128)S(1)}, f32[32,128]{1,0:T(8,128)S(1)}, f32[2,256,32]{2,0,1:T(2,128)S(1)}, s32[]{:T(128)}, /*index=5*/s32[32]...) while((s32[]{:T(128)}, f32[32,128]{1,0:T(8,128)S(1)}, ...), condition=%wide.region_40.39_spmd, body=%wide.region_7.38_spmd.sunk | while | flops 662181 | bytes 806215 | solution.py:133
  135.1 35.1 %while.96 = (s32[]{:T(128)}, f32[32,128]{1,0:T(8,128)S(1)}, f32[32,128]{1,0:T(8,128)S(1)}, f32[2,256,32]{2,0,1:T(2,128)S(1)}, s32[]{:T(128)}, /*index=5*/s32[32]...) while((s32[]{:T(128)}, f32[32,128]{1,0:T(8,128)S(1)}, ...), condition=%wide.region_40.39_spmd, body=%wide.region_7.38_spmd.sunk | while | flops 662181 | bytes 806215 | solution.py:133
  171.3 35.1 %while.96 = (s32[]{:T(128)}, f32[32,128]{1,0:T(8,128)S(1)}, f32[32,128]{1,0:T(8,128)S(1)}, f32[2,256,32]{2,0,1:T(2,128)S(1)}, s32[]{:T(128)}, /*index=5*/s32[32]...) while((s32[]{:T(128)}, f32[32,128]{1,0:T(8,128)S(1)}, ...), condition=%wide.region_40.39_spmd, body=%wide.region_7.38_spmd.sunk | while | flops 662181 | bytes 806215 | solution.py:133
  207.5 35.1 %while.96 = (s32[]{:T(128)}, f32[32,128]{1,0:T(8,128)S(1)}, f32[32,128]{1,0:T(8,128)S(1)}, f32[2,256,32]{2,0,1:T(2,128)S(1)}, s32[]{:T(128)}, /*index=5*/s32[32]...) while((s32[]{:T(128)}, f32[32,128]{1,0:T(8,128)S(1)}, ...), condition=%wide.region_40.39_spmd, body=%wide.region_7.38_spmd.sunk | while | flops 662181 | bytes 806215 | solution.py:133
  243.6 35.1 %while.96 = (s32[]{:T(128)}, f32[32,128]{1,0:T(8,128)S(1)}, f32[32,128]{1,0:T(8,128)S(1)}, f32[2,256,32]{2,0,1:T(2,128)S(1)}, s32[]{:T(128)}, /*index=5*/s32[32]...) while((s32[]{:T(128)}, f32[32,128]{1,0:T(8,128)S(1)}, ...), condition=%wide.region_40.39_spmd, body=%wide.region_7.38_spmd.sunk | while | flops 662181 | bytes 806215 | solution.py:133
  279.8 35.1 %while.96 = (s32[]{:T(128)}, f32[32,128]{1,0:T(8,128)S(1)}, f32[32,128]{1,0:T(8,128)S(1)}, f32[2,256,32]{2,0,1:T(2,128)S(1)}, s32[]{:T(128)}, /*index=5*/s32[32]...) while((s32[]{:T(128)}, f32[32,128]{1,0:T(8,128)S(1)}, ...), condition=%wide.region_40.39_spmd, body=%wide.region_7.38_spmd.sunk | while | flops 662181 | bytes 806215 | solution.py:133
  315.9 35.1 %while.96 = (s32[]{:T(128)}, f32[32,128]{1,0:T(8,128)S(1)}, f32[32,128]{1,0:T(8,128)S(1)}, f32[2,256,32]{2,0,1:T(2,128)S(1)}, s32[]{:T(128)}, /*index=5*/s32[32]...) while((s32[]{:T(128)}, f32[32,128]{1,0:T(8,128)S(1)}, ...), condition=%wide.region_40.39_spmd, body=%wide.region_7.38_spmd.sunk | while | flops 662181 | bytes 806215 | solution.py:133
  352.1 35.1 %while.96 = (s32[]{:T(128)}, f32[32,128]{1,0:T(8,128)S(1)}, f32[32,128]{1,0:T(8,128)S(1)}, f32[2,256,32]{2,0,1:T(2,128)S(1)}, s32[]{:T(128)}, /*index=5*/s32[32]...) while((s32[]{:T(128)}, f32[32,128]{1,0:T(8,128)S(1)}, ...), condition=%wide.region_40.39_spmd, body=%wide.region_7.38_spmd.sunk | while | flops 662181 | bytes 806215 | solution.py:133
  388.3 35.1 %while.96 = (s32[]{:T(128)}, f32[32,128]{1,0:T(8,128)S(1)}, f32[32,128]{1,0:T(8,128)S(1)}, f32[2,256,32]{2,0,1:T(2,128)S(1)}, s32[]{:T(128)}, /*index=5*/s32[32]...) while((s32[]{:T(128)}, f32[32,128]{1,0:T(8,128)S(1)}, ...), condition=%wide.region_40.39_spmd, body=%wide.region_7.38_spmd.sunk | while | flops 662181 | bytes 806215 | solution.py:133
  424.4 35.1 %while.96 = (s32[]{:T(128)}, f32[32,128]{1,0:T(8,128)S(1)}, f32[32,128]{1,0:T(8,128)S(1)}, f32[2,256,32]{2,0,1:T(2,128)S(1)}, s32[]{:T(128)}, /*index=5*/s32[32]...) while((s32[]{:T(128)}, f32[32,128]{1,0:T(8,128)S(1)}, ...), condition=%wide.region_40.39_spmd, body=%wide.region_7.38_spmd.sunk | while | flops 662181 | bytes 806215 | solution.py:133
  460.6 35.1 %while.96 = (s32[]{:T(128)}, f32[32,128]{1,0:T(8,128)S(1)}, f32[32,128]{1,0:T(8,128)S(1)}, f32[2,256,32]{2,0,1:T(2,128)S(1)}, s32[]{:T(128)}, /*index=5*/s32[32]...) while((s32[]{:T(128)}, f32[32,128]{1,0:T(8,128)S(1)}, ...), condition=%wide.region_40.39_spmd, body=%wide.region_7.38_spmd.sunk | while | flops 662181 | bytes 806215 | solution.py:133
  496.7 35.1 %while.96 = (s32[]{:T(128)}, f32[32,128]{1,0:T(8,128)S(1)}, f32[32,128]{1,0:T(8,128)S(1)}, f32[2,256,32]{2,0,1:T(2,128)S(1)}, s32[]{:T(128)}, /*index=5*/s32[32]...) while((s32[]{:T(128)}, f32[32,128]{1,0:T(8,128)S(1)}, ...), condition=%wide.region_40.39_spmd, body=%wide.region_7.38_spmd.sunk | while | flops 662181 | bytes 806215 | solution.py:133
  532.9 35.1 %while.96 = (s32[]{:T(128)}, f32[32,128]{1,0:T(8,128)S(1)}, f32[32,128]{1,0:T(8,128)S(1)}, f32[2,256,32]{2,0,1:T(2,128)S(1)}, s32[]{:T(128)}, /*index=5*/s32[32]...) while((s32[]{:T(128)}, f32[32,128]{1,0:T(8,128)S(1)}, ...), condition=%wide.region_40.39_spmd, body=%wide.region_7.38_spmd.sunk | while | flops 662181 | bytes 806215 | solution.py:133
  569.1 35.1 %while.96 = (s32[]{:T(128)}, f32[32,128]{1,0:T(8,128)S(1)}, f32[32,128]{1,0:T(8,128)S(1)}, f32[2,256,32]{2,0,1:T(2,128)S(1)}, s32[]{:T(128)}, /*index=5*/s32[32]...) while((s32[]{:T(128)}, f32[32,128]{1,0:T(8,128)S(1)}, ...), condition=%wide.region_40.39_spmd, body=%wide.region_7.38_spmd.sunk | while | flops 662181 | bytes 806215 | solution.py:133
  605.2 35.1 %while.96 = (s32[]{:T(128)}, f32[32,128]{1,0:T(8,128)S(1)}, f32[32,128]{1,0:T(8,128)S(1)}, f32[2,256,32]{2,0,1:T(2,128)S(1)}, s32[]{:T(128)}, /*index=5*/s32[32]...) while((s32[]{:T(128)}, f32[32,128]{1,0:T(8,128)S(1)}, ...), condition=%wide.region_40.39_spmd, body=%wide.region_7.38_spmd.sunk | while | flops 662181 | bytes 806215 | solution.py:133
  641.2 124.3 %dynamic_update_slice.38 = f32[64,2,4096]{0,1,2:T(2,128)} dynamic-update-slice(f32[64,2,4096]{0,1,2:T(2,128)} %get-tuple-element.2217, f32[32,2,4096]{0,1,2:T(2,128)} %get-tuple-element.1827, s32[]{:T(128)S(6)} %select_n.675, s32[]{:T(128)} %constant.607.clone.1..sunk, s32[]{:T(128)} %constant.607.clone.1..sunk) | dynamic-update-slice | bytes 2097156 | tf_op jit(solution)/shard_map/while/body/eval_jaxpr/dynamic_update_slice | solution.py:154
  772.5 578.5 %while.95 = (s32[]{:T(128)}, f32[32,128]{1,0:T(8,128)S(1)}, f32[32,128]{1,0:T(8,128)S(1)}, f32[32,2,4096]{0,1,2:T(2,128)}, s32[32]{0:T(128)S(1)}, /*index=5*/f32...) while((s32[]{:T(128)}, f32[32,128]{1,0:T(8,128)S(1)}, ...), condition=%wide.region_41.41_spmd.clone, body=%wide.region_6.40_spmd.clone.sunk | while | flops 686763 | bytes 1217226 | solution.py:140
  772.7 35.1 %while.96 = (s32[]{:T(128)}, f32[32,128]{1,0:T(8,128)S(1)}, f32[32,128]{1,0:T(8,128)S(1)}, f32[2,256,32]{2,0,1:T(2,128)S(1)}, s32[]{:T(128)}, /*index=5*/s32[32]...) while((s32[]{:T(128)}, f32[32,128]{1,0:T(8,128)S(1)}, ...), condition=%wide.region_40.39_spmd, body=%wide.region_7.38_spmd.sunk | while | flops 662181 | bytes 806215 | solution.py:133
  1351.0 674.8 %dynamic_update_slice.38 = f32[64,2,4096]{0,1,2:T(2,128)} dynamic-update-slice(f32[64,2,4096]{0,1,2:T(2,128)} %get-tuple-element.2217, f32[32,2,4096]{0,1,2:T(2,128)} %get-tuple-element.1827, s32[]{:T(128)S(6)} %select_n.675, s32[]{:T(128)} %constant.607.clone.1..sunk, s32[]{:T(128)} %constant.607.clone.1..sunk) | dynamic-update-slice | bytes 2097156 | tf_op jit(solution)/shard_map/while/body/eval_jaxpr/dynamic_update_slice | solution.py:154
  2025.9 108.2 %all-reduce.3.cloned.1.call-done = f32[64,2,4096]{0,1,2:T(2,128)} async-done(((f32[64,2,4096]{0,1,2:T(2,128)}), f32[64,2,4096]{0,1,2:T(2,128)}) %all-reduce.3.cloned.1.call-update) | async-done | bytes 2097168 | tf_op jit(solution)/shard_map/psum | solution.py:225
  2141.0 322.4 %psum.15 = f32[4096]{0:T(1024)S(1)} all-reduce(f32[4096]{0:T(1024)S(1)} %multiply_reduce_fusion), channel_id=1, replica_groups=mesh['blk'=2,'mblk'=64] {'mblk'}, use_global_device_ids=true, to_apply=%region_45.46 | all-reduce | flops 4096 | bytes 32768 | tf_op jit(solution)/shard_map/psum | solution.py:226
  (14526 shorter events, 1613.7 us)
Async XLA Ops:
  11.1 7.0 all-to-all-start
  18.1 6.7 all-to-all-start.1
  28.6 22.6 all-to-all-start.2
  41.7 2092.4 %all-reduce.3.cloned.1.call-start = ((), (), s32[]{:S(2)}) async-start(), calls=%async_computation.3 | async-start | bytes 8388608 | tf_op jit(solution)/shard_map/psum | solution.py:225
  2025.9 437.5 %copy-start = (f32[4096]{0:T(1024)S(1)}, f32[4096]{0:T(1024)}, u32[]{:S(2)}) copy-start(f32[4096]{0:T(1024)} %param.13) | copy-start | bytes 49156
Sparse Core Ops, SparseCore 0:
  2026.0 108.0 all-reduce.2
where the time goes:
time: 2480 us; the launch traced here: 2470 us
  other arithmetic  1030 us (42%)
  local copies, waits for them, and re-layouts  824 us (33%)
  blocking collectives  322 us (13%)
  loops' own time  141 us (6%)
  waiting for transfers between devices  121 us (5%)
    dynamic_update_slice x2, local copies, waits for them, and re-layouts, one_group(): lax.dynamic_update_slice_in_dim(result, group_rows, group_idx * group_siz...  799 us
    reduce_sum x1536, other arithmetic, sixteen_rows(): jnp.sum(fresh_row * spec_rows[0], axis=1)  566 us
    psum x1, blocking collectives, on_device(): power_sum = lax.psum(power_part(alm_rows, orders), 'mblk')  322 us
    select_n x1536, other arithmetic, advance_rows(): jnp.where(degree > orders[:, None], grown, jnp.where(degree == orders[:,...  194 us
    another operation x32, loops' own time, one_block(): lax.fori_loop(0, block_len // 16, sixteen_rows, (prev_one, prev_two, empt...  135 us
    while x7680, other arithmetic  116 us
    psum x1, waiting for transfers between devices, on_device(): alm_rows = lax.psum(partial_alm, 'blk')  108 us
    mul x2048, other arithmetic, coefficients(): alpha_term * jnp.sqrt(jnp.maximum((degree_f - 1.0 - orders_f) * (degree_f...  69 us

commit v1 on v0

v1 whole, which is shorter than its diff:
```python
import functools
import math

import jax
import jax.numpy as jnp
import numpy as np
from jax import lax
from jax.experimental import pallas as pl
from jax.experimental.pallas import tpu as pltpu
from jax.sharding import PartitionSpec as P

NSIDE = 2048
CYCLE_PIX = 8192
LMAX = 4096
BLOCK_PIX = 1024
CYCLES = 256
DEVICES = 128
MESH = pl.DeviceIdType.MESH
HIGHEST = lax.Precision.HIGHEST
F32 = jnp.float32


def dft_tables():
    k1 = np.arange(64)
    part, seg = np.meshgrid(np.arange(8), np.arange(8), indexing="ij")
    outer = (8 * seg + part).reshape(-1)
    angle = 2.0 * np.pi * ((k1[:, None] * outer[None, :]) % 64) / 64
    stage_one = np.concatenate([np.cos(angle), -np.sin(angle)], axis=0)
    inner = np.arange(128)
    twists = []
    stage_two = []
    upper = np.concatenate([np.arange(32), 63 - np.arange(32)])
    for cycle in range(2):
        shift = 0.5 if cycle == 0 else 0.0
        turn = 2.0 * np.pi * (k1[:, None] * (inner[None, :] + shift)) / CYCLE_PIX
        twists.append(np.stack([np.cos(turn), np.sin(turn)]))
        turn = 2.0 * np.pi * (upper[:, None] * inner[None, :] % 128) / 128 + (
            2.0 * np.pi * upper[:, None] * shift / 128
        )
        cos_two, sin_two = np.cos(turn), np.sin(turn)
        stage_two.append(
            np.concatenate(
                [
                    np.concatenate([cos_two, sin_two], axis=1),
                    np.concatenate([-sin_two, cos_two], axis=1),
                ],
                axis=0,
            )
        )
    return (
        stage_one.astype(np.float32),
        np.stack(twists).astype(np.float32),
        np.stack(stage_two).astype(np.float32),
    )


def half_logs():
    lat = (CYCLES // 2 - np.arange(CYCLES)) * (2.0 / (3.0 * NSIDE))
    return (0.5 * np.log1p(-lat * lat)).astype(np.float32)


def ratio_table():
    steps = np.arange(1, 4200, dtype=np.float64)
    prods = np.concatenate([[1.0], np.cumprod((2.0 * steps - 1.0) / (2.0 * steps))])
    j = np.arange(8384)
    even = 1.0 / (np.maximum(j, 1) * prods[j // 2])
    odd = prods[np.maximum(j - 1, 0) // 2]
    f = np.where(j % 2 == 0, even, odd)
    f[0] = 1.0
    return f


def degree_tables():
    f = ratio_table()
    step, lane = np.arange(128) // 16, np.arange(128) % 16
    diff = 8 * np.arange(528)[:, None] + (step - lane)[None, :]
    low = np.where(diff >= 0, f[np.maximum(diff, 0)], 0.0)
    high = f[8 * np.arange(1040)[:, None] + (step + lane)[None, :]]
    return low.astype(np.float32), high.astype(np.float32)


def fold_matrix():
    out = np.zeros((2, 2, 64, 128))
    for u in range(64):
        for c in range(2):
            south = 65 + u if c == 0 else 64 + u
            for odd in range(2):
                out[odd, c, u, 63 - u] += 1.0
                if south < 128:
                    out[odd, c, u, south] += -1.0 if odd else 1.0
    arrival = np.arange(128)
    y_source, x_source = arrival // 8, arrival % 8
    owner = (x_source // 4) * 64 + y_source * 4 + x_source % 4
    return out.reshape(256, 128)[:, owner].astype(np.float32)


EQUATOR_ROW = 4


def fourier_body(owner, own_ref, own_ids_ref, own_mask_ref, got_ref, got_ids_ref, got_mask_ref, one_ref, twist_ref, two_ref, logs_ref, out_ref):
    slot = lax.broadcasted_iota(jnp.int32, (16, 16), 0) + owner * 16
    pick_own = jnp.where(own_ids_ref[...] == slot, own_mask_ref[...], 0).astype(F32)
    pick_got = jnp.where(got_ids_ref[...] == slot, got_mask_ref[...], 0).astype(F32)
    rows = jnp.dot(pick_own, own_ref[...], precision=HIGHEST, preferred_element_type=F32) + jnp.dot(
        pick_got, got_ref[...], precision=HIGHEST, preferred_element_type=F32
    )
    folded = jnp.concatenate(
        [
            jnp.concatenate([rows[8 * c : 8 * c + 8, 128 * p : 128 * p + 128] for p in range(8)], axis=0)
            for c in range(2)
        ],
        axis=1,
    )
    first = jnp.dot(one_ref[...], folded, precision=HIGHEST, preferred_element_type=F32)
    k1 = lax.broadcasted_iota(jnp.int32, (64, 64), 1)
    row = lax.broadcasted_iota(jnp.int32, (64, 64), 0)
    orders = (k1 + 64 * jnp.where(row < 32, row, 95 - row)).astype(F32)
    outs = []
    for c in range(2):
        re, im = first[0:64, 128 * c : 128 * c + 128], first[64:128, 128 * c : 128 * c + 128]
        cos, sin = twist_ref[c, 0], twist_ref[c, 1]
        turned = jnp.concatenate([re * cos + im * sin, im * cos - re * sin], axis=1)
        spec = lax.dot_general(
            two_ref[c], turned, (((1,), (1,)), ((), ())), precision=HIGHEST, preferred_element_type=F32
        )
        seed = jnp.exp(orders * logs_ref[owner * 2 + c])
        outs.append((spec[0:64] * seed, spec[64:128] * seed))
    for j in range(4):
        pieces = []
        for ri in range(2):
            for half in range(2):
                jj = j if half == 0 else 3 - j
                for c in range(2):
                    pieces.append(outs[c][ri][32 * half : 32 * half + 32, 16 * jj : 16 * jj + 16])
        out_ref[2 * j : 2 * j + 2] = jnp.concatenate(pieces, axis=1).reshape(2, 16, 128)


def tables_body(d, low_ref, high_ref, coef_ref, gain_ref):
    row = lax.broadcasted_iota(jnp.int32, (8, 128), 0)
    lane = lax.broadcasted_iota(jnp.int32, (8, 128), 1)
    order = lane % 16
    offset = 8 * row + lane // 16
    picks = [order + 16 * step for step in range(8)]
    for half in range(2):
        first = 16 * d if half == 0 else 4080 - 16 * d
        start = 0 if half == 0 else 512 - 2 * d
        count = (4096 - first + 63) // 64

        def one(k, carry):
            low = low_ref[pl.ds(pl.multiple_of(8 * k, 8), 8), :]
            high = high_ref[pl.ds(first // 4 + 8 * k, 8), :]
            both = low * high
            t = offset + 64 * k
            degree = t + first
            down = t - order
            up = (degree + first + order).astype(F32)
            coef = both * (2 * degree - 1).astype(F32)
            weight = jnp.where(first + order == 0, 1.0, 2.0) * (1.0 / (CYCLES * CYCLE_PIX))
            denom = jnp.maximum(down.astype(F32), 1.0) * jnp.maximum(up, 1.0) * both
            gain = jnp.where(down >= 0, weight / jnp.where(down >= 0, denom, 1.0), 0.0)
            at = start + 8 * k
            for step in range(8):
                coef_ref[step, pl.ds(at, 8), :] = jnp.take_along_axis(
                    coef, picks[step], axis=1, mode="promise_in_bounds"
                )
                gain_ref[half, pl.ds(first + 64 * k + step, 8, stride=8), :] = jnp.take_along_axis(
                    gain, picks[step], axis=1, mode="promise_in_bounds"
                )
            return carry

        lax.fori_loop(0, count, one, 0)


def prepare(got_ref, fold_ref, state_ref):
    row = lax.broadcasted_iota(jnp.int32, (64, 128), 0)
    lane = lax.broadcasted_iota(jnp.int32, (64, 128), 1)
    folded = jnp.dot(fold_ref[...], got_ref[...], precision=HIGHEST, preferred_element_type=F32)
    is_c0 = (lane % 32) < 16
    even = jnp.where(is_c0, folded[0:64], folded[64:128])
    odd = jnp.where(is_c0, folded[128:192], folded[192:256])
    same = (lane % 2) == 0
    by_parity = (jnp.where(same, even, odd), jnp.where(same, odd, even))
    group = lax.broadcasted_iota(jnp.int32, (8, 128), 1) // 32
    for half in range(2):
        for p in range(2):
            for ri in range(2):
                source = 2 * ri + half
                for v in range(2):
                    total = None
                    for h in range(4):
                        piece = by_parity[p][32 * v + 8 * h : 32 * v + 8 * h + 8]
                        moved = pltpu.roll(piece, (32 * (h - source)) % 128, 1)
                        total = moved if total is None else jnp.where(group == h, moved, total)
                    state_ref[half, 4 * p + 2 * ri + v] = total
    step = lax.broadcasted_iota(jnp.int32, (8, 128), 0)
    lane8 = lax.broadcasted_iota(jnp.int32, (8, 128), 1)
    turn = (step - lane8 % 16) & 3
    sign = jnp.where(turn == 0, 1.0, jnp.where(turn == 2, -1.0, 0.0))
    line = jnp.broadcast_to(got_ref[EQUATOR_ROW : EQUATOR_ROW + 1, :], (8, 128))
    for half in range(2):
        for ri in range(2):
            source = 2 * ri + half
            base = jnp.where(lane8 // 16 == 2 * source, line, 0.0)
            base = base + pltpu.roll(base, 64, 1)
            base = base + pltpu.roll(base, 32, 1)
            base = base + pltpu.roll(base, 16, 1)
            state_ref[half, 8 + ri] = base * sign


def first_order(d, half):
    return 16 * d if half == 0 else 4080 - 16 * d


UNROLL = 8


def legendre_body(d, coef_ref, state_ref, raw_ref):
    row = lax.broadcasted_iota(jnp.int32, (8, 128), 0)
    lane = lax.broadcasted_iota(jnp.int32, (8, 128), 1)
    order = lane % 16
    masks = ((row & 1) == 0, (row & 2) == 0, (row & 4) == 0)
    lats = []
    for v in range(2):
        u = 32 * v + 8 * (lane // 32) + row
        q = 2 * u + jnp.where((lane % 32) < 16, 2, 1)
        lats.append(q.astype(F32) * (2.0 / (3.0 * NSIDE)))

    def merge(level, first, second):
        mask = masks[level]
        shift = 8 - (1 << level)
        return jnp.where(mask, first, second) + pltpu.roll(jnp.where(mask, second, first), shift, 0)

    def eight(half, base, lead, weights, state, seeded, k):
        a0, a1, b0, b1 = state
        stack = {}
        for step in range(8):
            coef = jnp.broadcast_to(coef_ref[step, pl.ds(base + k, 1), :], (8, 128))
            n0 = (coef * lats[0]) * a0 - b0
            n1 = (coef * lats[1]) * a1 - b1
            if seeded is not None:
                start = order == (seeded * 8 + step)
                n0 = jnp.where(start, 1.0, n0)
                n1 = jnp.where(start, 1.0, n1)
            a0, a1, b0, b1 = n0, n1, a0, a1
            p = step % 2
            for ri in range(2):
                term = n0 * weights[4 * p + 2 * ri] + n1 * weights[4 * p + 2 * ri + 1]
                level, idx = 0, step
                while idx % 2 == 1:
                    term = merge(level, stack.pop((ri, level)), term)
                    level, idx = level + 1, idx // 2
                stack[(ri, level)] = term
        for ri in range(2):
            raw_ref[half, ri, lead + k] = stack[(ri, 3)]
        return (a0, a1, b0, b1)

    for half in range(2):
        first = first_order(d, half)
        base = 0 if half == 0 else 512 - 2 * d
        lead = first // 8
        weights = [state_ref[half, n] for n in range(8)]
        zero = jnp.zeros((8, 128), F32)
        for ri in range(2):
            raw_ref[half, ri, pl.ds(first // 128 * 16, 16)] = jnp.zeros((16, 8, 128), F32)
        state = (zero, zero, zero, zero)
        for k in range(2):
            state = eight(half, base, lead, weights, state, k, k)
        def many(n, state):
            for k in range(UNROLL):
                state = eight(half, base, lead, weights, state, None, UNROLL * n + k + 2)
            return state

        lax.fori_loop(0, ((4096 - first) // 8 - 2 + UNROLL - 1) // UNROLL, many, state)


def clear_gain(d, gain_ref):
    for half in range(2):
        tile = pl.multiple_of(first_order(d, half) // 128 * 128, 128)
        gain_ref[half, pl.ds(tile, 128), :] = jnp.zeros((128, 128), F32)


def power_body(d, raw_ref, gain_ref, state_ref, power_ref):
    ones = jnp.full((8, 128), 0.125, F32)
    power_ref[...] = jnp.zeros_like(power_ref)
    for half in range(2):
        equator = [jnp.concatenate([state_ref[half, 8 + ri]] * 16, axis=0) for ri in range(2)]

        def one(tile, carry):
            total = None
            for ri in range(2):
                value = raw_ref[half, ri, pl.ds(16 * tile, 16)].reshape(128, 128)
                for shift in (64, 32, 16):
                    value = value + pltpu.roll(value, shift, 1)
                value = value + equator[ri]
                total = value * value if total is None else total + value * value
            total = total * gain_ref[half, pl.ds(pl.multiple_of(128 * tile, 128), 128), :]
            power_ref[tile] = power_ref[tile] + lax.dot_general(
                ones, total, (((1,), (1,)), ((), ())), precision=HIGHEST, preferred_element_type=F32
            )
            return carry

        lax.fori_loop(first_order(d, half) // 128, 32, one, 0)


def position():
    blk, mblk = lax.axis_index("blk"), lax.axis_index("mblk")
    return blk * 4 + mblk % 4, mblk // 4


def device_at(x, y):
    return (x // 4, y * 4 + x % 4)


def order_block(rank):
    return 4 * (rank % 32) + rank // 32


def greet(x, y):
    barrier = pltpu.get_barrier_semaphore()
    for step in range(1, 8):
        pl.semaphore_signal(barrier, inc=1, device_id=device_at((x + step) % 8, y), device_id_type=MESH)
    for step in range(1, 16):
        pl.semaphore_signal(barrier, inc=1, device_id=device_at(x, (y + step) % 16), device_id_type=MESH)
    pl.semaphore_wait(barrier, 22)


def send(source, target, send_sem, recv_sem, device):
    copy = pltpu.make_async_remote_copy(
        src_ref=source, dst_ref=target, send_sem=send_sem, recv_sem=recv_sem, device_id=device, device_id_type=MESH
    )
    copy.start()
    return copy


def drain(ref, sem):
    pltpu.make_async_copy(ref, ref, sem).wait()


def fourier_kernel(
    own_ref, own_ids_ref, own_mask_ref, one_ref, twist_ref, two_ref, logs_ref, out_ref,
    got_ref, got_ids_ref, got_mask_ref, rows_ref, mid_ref, again_ref, land_ref, pair_send, pair_recv, send_sem, recv_sem,
):
    x, y = position()
    greet(x, y)
    partner = device_at((x + 4) % 8, y)
    pair = [
        send(source, target, pair_send.at[n], pair_recv.at[n], partner)
        for n, (source, target) in enumerate(
            ((own_ref, got_ref), (own_ids_ref, got_ids_ref), (own_mask_ref, got_mask_ref))
        )
    ]
    for copy in pair:
        copy.wait()
    owner = (x // 4) * 64 + y * 4 + x % 4
    fourier_body(
        owner, own_ref, own_ids_ref, own_mask_ref, got_ref, got_ids_ref, got_mask_ref,
        one_ref, twist_ref, two_ref, logs_ref, rows_ref,
    )
    for step in range(1, 8):
        to = (x + step) % 8
        send(rows_ref.at[to], mid_ref.at[x], send_sem.at[0], recv_sem.at[0], device_at(to, y))
    mid_ref[x] = rows_ref[x]
    drain(mid_ref.at[pl.ds(0, 7)], recv_sem.at[0])
    every = mid_ref[...]
    for to in range(16):
        again_ref[to] = jnp.concatenate([every[n, to : to + 1, :] for n in range(8)], axis=0)
    for step in range(1, 16):
        to = (y + step) % 16
        send(again_ref.at[to], land_ref.at[y], send_sem.at[1], recv_sem.at[1], device_at(x, to))
    land_ref[y] = again_ref[y]
    drain(land_ref.at[pl.ds(0, 15)], recv_sem.at[1])
    out_ref[...] = land_ref[...].reshape(128, 128)
    drain(mid_ref.at[pl.ds(0, 7)], send_sem.at[0])
    drain(land_ref.at[pl.ds(0, 15)], send_sem.at[1])


def reduce_kernel(power_ref, model_ref, pseudo_ref, misfit_ref, part_ref, first_ref, second_ref, third_ref, send_sem, recv_sem):
    x, y = position()
    greet(x, y)
    part_ref[...] = jnp.zeros_like(part_ref)
    for n in range(8):
        part_ref[n, 0:4, :] = power_ref[4 * n : 4 * n + 4, :]
    for step in range(1, 8):
        to = (x + step) % 8
        send(part_ref.at[to], first_ref.at[x], send_sem.at[0], recv_sem.at[0], device_at(to, y))
    first_ref[x] = part_ref[x]
    drain(first_ref.at[pl.ds(0, 7)], recv_sem.at[0])
    second_ref[y] = jnp.sum(first_ref[...], axis=0)
    for step in range(1, 16):
        to = (y + step) % 16
        send(second_ref.at[y], second_ref.at[y], send_sem.at[1], recv_sem.at[1], device_at(x, to))
    drain(second_ref.at[pl.ds(0, 15)], recv_sem.at[1])
    third_ref[x] = jnp.sum(second_ref[...], axis=0)
    for step in range(1, 8):
        to = (x + step) % 8
        send(third_ref.at[x], third_ref.at[x], send_sem.at[2], recv_sem.at[2], device_at(to, y))
    drain(third_ref.at[pl.ds(0, 7)], recv_sem.at[2])
    total = jnp.zeros((1, 1), F32)
    for n in range(8):
        pseudo = third_ref[n, 0:4, :]
        model = model_ref[4 * n : 4 * n + 4, :]
        pseudo_ref[4 * n : 4 * n + 4, :] = pseudo
        rel_error = (pseudo - model) / model
        total = total + jnp.sum(rel_error * rel_error, keepdims=True)
    misfit_ref[...] = total * (1.0 / LMAX)
    drain(first_ref.at[pl.ds(0, 7)], send_sem.at[0])
    drain(second_ref.at[pl.ds(0, 15)], send_sem.at[1])
    drain(third_ref.at[pl.ds(0, 7)], send_sem.at[2])


def legendre_kernel(got_ref, fold_ref, low_ref, high_ref, out_ref, coef_ref, gain_ref, state_ref, raw_ref, power_ref):
    x, y = position()
    d = order_block(x * 16 + y)
    clear_gain(d, gain_ref)
    tables_body(d, low_ref, high_ref, coef_ref, gain_ref)
    prepare(got_ref, fold_ref, state_ref)
    legendre_body(d, coef_ref, state_ref, raw_ref)
    power_body(d, raw_ref, gain_ref, state_ref, power_ref)
    out_ref[...] = power_ref[:, 0, :]


LEGENDRE_SCRATCH = lambda: [
    pltpu.VMEM((8, 544, 128), F32),
    pltpu.VMEM((2, 4096 + 64, 128), F32),
    pltpu.VMEM((2, 10, 8, 128), F32),
    pltpu.VMEM((2, 2, 512 + 16, 8, 128), F32),
    pltpu.VMEM((32, 8, 128), F32),
]
VM = pl.BlockSpec(memory_space=pltpu.VMEM)
SM = pl.BlockSpec(memory_space=pltpu.SMEM)


def on_device(pixels, block_ids, block_mask, model_cl):
    one, twist, two = dft_tables()
    dma = pltpu.SemaphoreType.DMA
    received = pl.pallas_call(
        fourier_kernel,
        out_shape=jax.ShapeDtypeStruct((DEVICES, 128), F32),
        in_specs=[VM] * 6 + [SM],
        out_specs=VM,
        scratch_shapes=[
            pltpu.VMEM((16, BLOCK_PIX), F32),
            pltpu.VMEM((1, 16), jnp.int32),
            pltpu.VMEM((1, 16), jnp.int32),
            pltpu.VMEM((8, 16, 128), F32),
            pltpu.VMEM((8, 16, 128), F32),
            pltpu.VMEM((16, 8, 128), F32),
            pltpu.VMEM((16, 8, 128), F32),
            dma((3,)),
            dma((3,)),
            dma((2,)),
            dma((2,)),
        ],
        compiler_params=pltpu.CompilerParams(collective_id=0, has_side_effects=True),
    )(pixels, block_ids.reshape(1, 16), block_mask.reshape(1, 16), one, twist, two, half_logs())
    low, high = degree_tables()
    power = pl.pallas_call(
        legendre_kernel,
        out_shape=jax.ShapeDtypeStruct((32, 128), F32),
        in_specs=[VM] * 4,
        out_specs=VM,
        scratch_shapes=LEGENDRE_SCRATCH(),
        compiler_params=pltpu.CompilerParams(vmem_limit_bytes=40 * 1024 * 1024),
    )(received, fold_matrix(), low, high)
    pseudo_cl, misfit = pl.pallas_call(
        reduce_kernel,
        out_shape=(jax.ShapeDtypeStruct((32, 128), F32), jax.ShapeDtypeStruct((1, 1), F32)),
        in_specs=[VM] * 2,
        out_specs=(VM, VM),
        scratch_shapes=[
            pltpu.VMEM((8, 8, 128), F32),
            pltpu.VMEM((8, 8, 128), F32),
            pltpu.VMEM((16, 8, 128), F32),
            pltpu.VMEM((8, 8, 128), F32),
            dma((3,)),
            dma((3,)),
        ],
        compiler_params=pltpu.CompilerParams(collective_id=1, has_side_effects=True),
    )(power, model_cl.reshape(32, 128))
    return pseudo_cl.reshape(LMAX), misfit.reshape(())


def solution(mesh):
    in_specs = (P(("blk", "mblk"), None), P(("blk", "mblk")), P(("blk", "mblk")), P())
    return jax.shard_map(on_device, mesh=mesh, in_specs=in_specs, out_specs=(P(), P()), check_vma=False)
```

time: 2480 us -> 80 us (0.03)
  other arithmetic: 1030 us -> 0 us
  local copies, waits for them, and re-layouts: 824 us -> 4.62 us
  blocking collectives: 322 us -> 0 us
  loops' own time: 141 us -> 0 us
  waiting for transfers between devices: 121 us -> 0 us
  Pallas kernels: 0 us -> 72.5 us
    dynamic_update_slice x514 -> x0, local copies, waits for them, and re-layouts: 806 us -> none  [the longest x2 799 us: one_group(): lax.dynamic_update_slice_in_dim(result, group_rows, group_idx * group_siz...]
    reduce_sum x1538 -> x0, other arithmetic: 568 us -> none  [the longest x1536 566 us: sixteen_rows(): jnp.sum(fresh_row * spec_rows[0], axis=1)]
    psum x1 -> x0, blocking collectives: 322 us -> none  [on_device(): power_sum = lax.psum(power_part(alm_rows, orders), 'mblk')]
    select_n x1542 -> x0, other arithmetic: 194 us -> none  [the longest x1536 194 us: advance_rows(): jnp.where(degree > orders[:, None], grown, jnp.where(degree == orders[:,...]
    another operation x35 -> x0, loops' own time: 141 us -> none  [the longest x32 135 us: one_block(): lax.fori_loop(0, block_len // 16, sixteen_rows, (prev_one, prev_two, empt...]
    while x7680 -> x0, other arithmetic: 116 us -> none
    psum x1 -> x0, waiting for transfers between devices: 108 us -> none  [on_device(): alm_rows = lax.psum(partial_alm, 'blk')]
    pallas_call x0 -> x3, Pallas kernels: none -> 72.5 us  [the longest x1 33.2 us: on_device(): pl.pallas_call(legendre_kernel, out_shape=jax.ShapeDtypeStruct((32, 128),...]
where the time goes in v1:
time: 80 us; the launch traced here: 79.6 us
  Pallas kernels  72.5 us (91%)
  local copies, waits for them, and re-layouts  4.62 us (6%)
  between operations  2.51 us (3%)
    pallas_call x1, Pallas kernels, on_device(): pl.pallas_call(legendre_kernel, out_shape=jax.ShapeDtypeStruct((32, 128),...  33.2 us
    pallas_call x1, Pallas kernels, on_device(): pl.pallas_call(fourier_kernel, out_shape=jax.ShapeDtypeStruct((DEVICES, 1...  22.4 us
    pallas_call x1, Pallas kernels, on_device(): pl.pallas_call(reduce_kernel, out_shape=(jax.ShapeDtypeStruct((32, 128),...  16.8 us
    unnamed x11, local copies, waits for them, and re-layouts  4.62 us

profile of v1, /device:TPU:1, one launch (start us, length us, event | category | flops | bytes accessed | tf_op | source)
XLA Modules:
  0.0 79.6 jit_solution(9709436455988364212)
XLA Ops:
  0.6 0.0 copy-start
  0.6 22.4 %shard_map.122.got_ref = f32[128,128]{1,0:T(8,128)} custom-call(f32[16,1024]{1,0:T(8,128)} %own_ref.1, s32[1,16]{1,0:T(1,128)} %bitcast.7, s32[1,16]{1,0:T(1,128)} %bitcast.8, f32[128,64]{1,0:T(8,128)} %constant.14.clone.one_ref, f32[2,2,64,128]{3,2,1,0:T(8,128)} %constant.15.clone.twist_ref, f32[2,128,256]{2,1,0:T(8,128)} %constant.16.clone.two_ref, ...), custom_call_target="tpu_custom_call" | custom-call | tf_op jit(solution)/shard_map/pallas_call | solution.py:436
  23.1 0.0 copy-done
  23.1 0.0 copy-start.1
  23.1 0.9 %copy-done.1 = f32[528,128]{1,0:T(8,128)S(1)} copy-done((f32[528,128]{1,0:T(8,128)S(1)}, f32[528,128]{1,0:T(8,128)}, u32[]{:S(2)}) %copy-start.1) | copy-done | bytes 270360
  24.1 0.0 copy-start.2
  24.1 0.8 %copy-done.2 = f32[128,128]{1,0:T(8,128)S(1)} copy-done((f32[128,128]{1,0:T(8,128)S(1)}, f32[128,128]{1,0:T(8,128)}, u32[]{:S(2)}) %copy-start.2) | copy-done | bytes 65560
  24.9 0.0 copy-start.3
  24.9 0.9 %copy-done.3 = f32[256,128]{1,0:T(8,128)S(1)} copy-done((f32[256,128]{1,0:T(8,128)S(1)}, f32[256,128]{1,0:T(8,128)}, u32[]{:S(2)}) %copy-start.3) | copy-done | bytes 131096
  25.8 33.2 %shard_map.123.power_ref = f32[32,128]{1,0:T(8,128)S(1)} custom-call(f32[128,128]{1,0:T(8,128)S(1)} %copy-done.2, f32[256,128]{1,0:T(8,128)S(1)} %copy-done.3, f32[528,128]{1,0:T(8,128)S(1)} %copy-done.1, f32[1040,128]{1,0:T(8,128)S(1)} %copy-done), custom_call_target="tpu_custom_call" | custom-call | tf_op jit(solution)/shard_map/pallas_call | solution.py:457
  59.0 0.0 copy-start.4
  59.0 0.6 copy-done.4
  59.6 16.8 %shard_map.124 = (f32[32,128]{1,0:T(8,128)}, f32[1,1]{1,0:T(1,128)}) custom-call(f32[32,128]{1,0:T(8,128)} %copy-done.4, f32[32,128]{1,0:T(8,128)} %bitcast.5), custom_call_target="tpu_custom_call" | custom-call | tf_op jit(solution)/shard_map/pallas_call | solution.py:465
  76.5 1.3 %copy.15 = f32[4096]{0:T(1024)} copy(f32[4096]{0:T(1024)} %bitcast.6) | data formatting | bytes 32768
Async XLA Ops:
  0.6 22.5 %copy-start = (f32[1040,128]{1,0:T(8,128)S(1)}, f32[1040,128]{1,0:T(8,128)}, u32[]{:S(2)}) copy-start(f32[1040,128]{1,0:T(8,128)} %constant.20.clone.high_ref) | copy-start | bytes 1597444
  23.1 1.0 %copy-start.1 = (f32[528,128]{1,0:T(8,128)S(1)}, f32[528,128]{1,0:T(8,128)}, u32[]{:S(2)}) copy-start(f32[528,128]{1,0:T(8,128)} %constant.19.clone.low_ref) | copy-start | bytes 811012
  24.1 0.8 %copy-start.2 = (f32[128,128]{1,0:T(8,128)S(1)}, f32[128,128]{1,0:T(8,128)}, u32[]{:S(2)}) copy-start(f32[128,128]{1,0:T(8,128)} %shard_map.122.got_ref) | copy-start | bytes 196612
  24.9 0.9 %copy-start.3 = (f32[256,128]{1,0:T(8,128)S(1)}, f32[256,128]{1,0:T(8,128)}, u32[]{:S(2)}) copy-start(f32[256,128]{1,0:T(8,128)} %constant.18.clone.fold_ref) | copy-start | bytes 393220
  59.0 0.6 copy-start.4

commit v2 on v1

--- a/solution.py
+++ b/solution.py
@@ -18,6 +18,10 @@
 MESH = pl.DeviceIdType.MESH
 HIGHEST = lax.Precision.HIGHEST
 F32 = jnp.float32
+BF16 = jnp.bfloat16
+ROWS = 544
+TILES = 33
+POWER_UNROLL = 3
 
 
 def dft_tables():
@@ -135,16 +139,35 @@
         out_ref[2 * j : 2 * j + 2] = jnp.concatenate(pieces, axis=1).reshape(2, 16, 128)
 
 
-def tables_body(d, low_ref, high_ref, coef_ref, gain_ref):
+def pieces_of(value):
+    high = value.astype(BF16)
+    rest = value - high.astype(F32)
+    middle = rest.astype(BF16)
+    return high, middle, (rest - middle.astype(F32)).astype(BF16)
+
+
+def lane_groups():
+    row = lax.broadcasted_iota(jnp.int32, (16, 128), 0)
+    lane = lax.broadcasted_iota(jnp.int32, (16, 128), 1)
+    return jnp.where(lane % 16 == row, 1.0, 0.0).astype(BF16)
+
+
+def grouped(groups, pieces):
+    total = None
+    for piece in pieces:
+        part = lax.dot_general(groups, piece, (((1,), (1,)), ((), ())), preferred_element_type=F32)
+        total = part if total is None else total + part
+    return total
+
+
+def compact_tables(d, low_ref, high_ref, coef_ref, gain_ref):
     row = lax.broadcasted_iota(jnp.int32, (8, 128), 0)
     lane = lax.broadcasted_iota(jnp.int32, (8, 128), 1)
     order = lane % 16
     offset = 8 * row + lane // 16
-    picks = [order + 16 * step for step in range(8)]
     for half in range(2):
-        first = 16 * d if half == 0 else 4080 - 16 * d
+        first = first_order(d, half)
         start = 0 if half == 0 else 512 - 2 * d
-        count = (4096 - first + 63) // 64
 
         def one(k, carry):
             low = low_ref[pl.ds(pl.multiple_of(8 * k, 8), 8), :]
@@ -154,27 +177,49 @@
             degree = t + first
             down = t - order
             up = (degree + first + order).astype(F32)
-            coef = both * (2 * degree - 1).astype(F32)
             weight = jnp.where(first + order == 0, 1.0, 2.0) * (1.0 / (CYCLES * CYCLE_PIX))
             denom = jnp.maximum(down.astype(F32), 1.0) * jnp.maximum(up, 1.0) * both
-            gain = jnp.where(down >= 0, weight / jnp.where(down >= 0, denom, 1.0), 0.0)
-            at = start + 8 * k
-            for step in range(8):
-                coef_ref[step, pl.ds(at, 8), :] = jnp.take_along_axis(
-                    coef, picks[step], axis=1, mode="promise_in_bounds"
-                )
-                gain_ref[half, pl.ds(first + 64 * k + step, 8, stride=8), :] = jnp.take_along_axis(
-                    gain, picks[step], axis=1, mode="promise_in_bounds"
-                )
+            at = pl.ds(start + 8 * k, 8)
+            coef_ref[at, :] = both * (2 * degree - 1).astype(F32)
+            gain_ref[at, :] = jnp.where(down >= 0, weight / jnp.where(down >= 0, denom, 1.0), 0.0)
             return carry
 
-        lax.fori_loop(0, count, one, 0)
+        lax.fori_loop(0, (4096 - first + 63) // 64, one, 0)
+
+
+def spread_coef(coef_ref, spread_ref, wide_ref):
+    spread = spread_ref[...]
+    for chunk in range(4):
+        at = pl.ds(ROWS // 4 * chunk, ROWS // 4)
+        total = None
+        for piece in pieces_of(coef_ref[at, :]):
+            part = jnp.dot(piece, spread, preferred_element_type=F32)
+            total = part if total is None else total + part
+        for step in range(8):
+            wide_ref[step, at, :] = total[:, 128 * step : 128 * step + 128]
+
+
+def spread_gain(gain_ref, turned_ref):
+    groups = lane_groups()
+    row = lax.broadcasted_iota(jnp.int32, (8, 128), 0)
+    lane = lax.broadcasted_iota(jnp.int32, (8, 128), 1)
+    same = lane // 16 == row
+
+    def one(tile, carry):
+        rows = [
+            jnp.where(same, jnp.broadcast_to(gain_ref[pl.ds(16 * tile + n, 1), :], (8, 128)), 0.0) for n in range(16)
+        ]
+        turned_ref[tile] = grouped(groups, pieces_of(jnp.concatenate(rows, axis=0)))
+        return carry
+
+    lax.fori_loop(0, TILES, one, 0)
 
 
 def prepare(got_ref, fold_ref, state_ref):
     row = lax.broadcasted_iota(jnp.int32, (64, 128), 0)
     lane = lax.broadcasted_iota(jnp.int32, (64, 128), 1)
-    folded = jnp.dot(fold_ref[...], got_ref[...], precision=HIGHEST, preferred_element_type=F32)
+    got = got_ref[...].reshape(128, 128)
+    folded = jnp.dot(fold_ref[...], got, precision=HIGHEST, preferred_element_type=F32)
     is_c0 = (lane % 32) < 16
     even = jnp.where(is_c0, folded[0:64], folded[64:128])
     odd = jnp.where(is_c0, folded[128:192], folded[192:256])
@@ -196,14 +241,12 @@
     lane8 = lax.broadcasted_iota(jnp.int32, (8, 128), 1)
     turn = (step - lane8 % 16) & 3
     sign = jnp.where(turn == 0, 1.0, jnp.where(turn == 2, -1.0, 0.0))
-    line = jnp.broadcast_to(got_ref[EQUATOR_ROW : EQUATOR_ROW + 1, :], (8, 128))
+    line = jnp.broadcast_to(got[EQUATOR_ROW : EQUATOR_ROW + 1, :], (8, 128))
     for half in range(2):
         for ri in range(2):
             source = 2 * ri + half
             base = jnp.where(lane8 // 16 == 2 * source, line, 0.0)
-            base = base + pltpu.roll(base, 64, 1)
-            base = base + pltpu.roll(base, 32, 1)
-            base = base + pltpu.roll(base, 16, 1)
+            base = pltpu.roll(base, (128 - 32 * source) % 128, 1)
             state_ref[half, 8 + ri] = base * sign
 
 
@@ -230,7 +273,7 @@
         shift = 8 - (1 << level)
         return jnp.where(mask, first, second) + pltpu.roll(jnp.where(mask, second, first), shift, 0)
 
-    def eight(half, base, lead, weights, state, seeded, k):
+    def eight(base, weights, state, seeded, k):
         a0, a1, b0, b1 = state
         stack = {}
         for step in range(8):
@@ -251,55 +294,53 @@
                     level, idx = level + 1, idx // 2
                 stack[(ri, level)] = term
         for ri in range(2):
-            raw_ref[half, ri, lead + k] = stack[(ri, 3)]
+            raw_ref[ri, base + k] = stack[(ri, 3)] + weights[8 + ri]
         return (a0, a1, b0, b1)
 
     for half in range(2):
         first = first_order(d, half)
         base = 0 if half == 0 else 512 - 2 * d
-        lead = first // 8
-        weights = [state_ref[half, n] for n in range(8)]
+        weights = [state_ref[half, n] for n in range(10)]
         zero = jnp.zeros((8, 128), F32)
-        for ri in range(2):
-            raw_ref[half, ri, pl.ds(first // 128 * 16, 16)] = jnp.zeros((16, 8, 128), F32)
         state = (zero, zero, zero, zero)
         for k in range(2):
-            state = eight(half, base, lead, weights, state, k, k)
+            state = eight(base, weights, state, k, k)
         def many(n, state):
             for k in range(UNROLL):
-                state = eight(half, base, lead, weights, state, None, UNROLL * n + k + 2)
+                state = eight(base, weights, state, None, UNROLL * n + k + 2)
             return state
 
         lax.fori_loop(0, ((4096 - first) // 8 - 2 + UNROLL - 1) // UNROLL, many, state)
 
 
-def clear_gain(d, gain_ref):
-    for half in range(2):
-        tile = pl.multiple_of(first_order(d, half) // 128 * 128, 128)
-        gain_ref[half, pl.ds(tile, 128), :] = jnp.zeros((128, 128), F32)
-
-
-def power_body(d, raw_ref, gain_ref, state_ref, power_ref):
-    ones = jnp.full((8, 128), 0.125, F32)
-    power_ref[...] = jnp.zeros_like(power_ref)
-    for half in range(2):
-        equator = [jnp.concatenate([state_ref[half, 8 + ri]] * 16, axis=0) for ri in range(2)]
-
-        def one(tile, carry):
-            total = None
-            for ri in range(2):
-                value = raw_ref[half, ri, pl.ds(16 * tile, 16)].reshape(128, 128)
-                for shift in (64, 32, 16):
-                    value = value + pltpu.roll(value, shift, 1)
-                value = value + equator[ri]
-                total = value * value if total is None else total + value * value
-            total = total * gain_ref[half, pl.ds(pl.multiple_of(128 * tile, 128), 128), :]
-            power_ref[tile] = power_ref[tile] + lax.dot_general(
-                ones, total, (((1,), (1,)), ((), ())), precision=HIGHEST, preferred_element_type=F32
-            )
-            return carry
-
-        lax.fori_loop(first_order(d, half) // 128, 32, one, 0)
+def power_body(d, raw_ref, turned_ref, rows_ref, shift_ref):
+    groups = lane_groups()
+
+    def one(tile, carry):
+        total = None
+        for ri in range(2):
+            value = raw_ref[ri, pl.ds(pl.multiple_of(16 * tile, 16), 16)].reshape(128, 128)
+            value = grouped(groups, pieces_of(value))
+            total = value * value if total is None else total + value * value
+        rows_ref[pl.ds(tile, 1), :] = jnp.sum(total * turned_ref[tile], axis=0, keepdims=True)
+        return carry
+
+    def several(n, carry):
+        for k in range(POWER_UNROLL):
+            one(POWER_UNROLL * n + k, carry)
+        return carry
+
+    lax.fori_loop(0, TILES // POWER_UNROLL, several, 0)
+    bound = 4096 - 16 * d
+    step = 128 * lax.broadcasted_iota(jnp.int32, (40, 128), 0) + lax.broadcasted_iota(jnp.int32, (40, 128), 1)
+    rows = rows_ref[...]
+    shift_ref[0:32, :] = jnp.zeros((32, 128), F32)
+    shift_ref[32:72, :] = pltpu.roll(jnp.where(step < bound, rows, 0.0), 16 * (d % 8), 1)
+    later = pltpu.roll(jnp.where((step >= bound) & (step < 4112), rows, 0.0), 112, 1)
+    lane = lax.broadcasted_iota(jnp.int32, (32, 128), 1)
+    near = shift_ref[pl.ds(32 - d // 8, 32), :]
+    far = shift_ref[pl.ds(31 - d // 8, 32), :]
+    return jnp.where(lane >= 16 * (d % 8), near, far) + jnp.where(lane < 112, later[0:32], later[1:33])
 
 
 def position():
@@ -336,12 +377,31 @@
     pltpu.make_async_copy(ref, ref, sem).wait()
 
 
-def fourier_kernel(
-    own_ref, own_ids_ref, own_mask_ref, one_ref, twist_ref, two_ref, logs_ref, out_ref,
-    got_ref, got_ids_ref, got_mask_ref, rows_ref, mid_ref, again_ref, land_ref, pair_send, pair_recv, send_sem, recv_sem,
+def everything(
+    own_ref, own_ids_ref, own_mask_ref, model_ref, logs_ref,
+    one_hbm, twist_hbm, two_hbm, low_hbm, high_hbm, spread_hbm, fold_hbm,
+    pseudo_ref, misfit_ref,
+    one_ref, twist_ref, two_ref, low_ref, high_ref, spread_ref, fold_ref, local_sem,
+    got_ref, got_ids_ref, got_mask_ref, rows_ref, mid_ref, again_ref, land_ref,
+    coef_ref, gain_ref, wide_ref, turned_ref, state_ref, raw_ref, sums_ref, shift_ref,
+    part_ref, first_ref, second_ref, third_ref,
+    pair_send, pair_recv, send_sem, recv_sem,
 ):
     x, y = position()
+    d = order_block(x * 16 + y)
+    owner = (x // 4) * 64 + y * 4 + x % 4
+    loads = [
+        pltpu.make_async_copy(source, target, local_sem.at[n])
+        for n, (source, target) in enumerate(
+            (
+                (one_hbm, one_ref), (twist_hbm, twist_ref), (two_hbm, two_ref), (low_hbm, low_ref),
+                (high_hbm, high_ref), (spread_hbm, spread_ref), (fold_hbm, fold_ref),
+            )
+        )
+    ]
     greet(x, y)
+    for copy in loads:
+        copy.start()
     partner = device_at((x + 4) % 8, y)
     pair = [
         send(source, target, pair_send.at[n], pair_recv.at[n], partner)
@@ -349,9 +409,11 @@
             ((own_ref, got_ref), (own_ids_ref, got_ids_ref), (own_mask_ref, got_mask_ref))
         )
     ]
+    for copy in loads:
+        copy.wait()
+    compact_tables(d, low_ref, high_ref, coef_ref, gain_ref)
     for copy in pair:
         copy.wait()
-    owner = (x // 4) * 64 + y * 4 + x % 4
     fourier_body(
         owner, own_ref, own_ids_ref, own_mask_ref, got_ref, got_ids_ref, got_mask_ref,
         one_ref, twist_ref, two_ref, logs_ref, rows_ref,
@@ -360,6 +422,7 @@
         to = (x + step) % 8
         send(rows_ref.at[to], mid_ref.at[x], send_sem.at[0], recv_sem.at[0], device_at(to, y))
     mid_ref[x] = rows_ref[x]
+    spread_coef(coef_ref, spread_ref, wide_ref)
     drain(mid_ref.at[pl.ds(0, 7)], recv_sem.at[0])
     every = mid_ref[...]
     for to in range(16):
@@ -368,33 +431,29 @@
         to = (y + step) % 16
         send(again_ref.at[to], land_ref.at[y], send_sem.at[1], recv_sem.at[1], device_at(x, to))
     land_ref[y] = again_ref[y]
+    spread_gain(gain_ref, turned_ref)
     drain(land_ref.at[pl.ds(0, 15)], recv_sem.at[1])
-    out_ref[...] = land_ref[...].reshape(128, 128)
-    drain(mid_ref.at[pl.ds(0, 7)], send_sem.at[0])
-    drain(land_ref.at[pl.ds(0, 15)], send_sem.at[1])
-
-
-def reduce_kernel(power_ref, model_ref, pseudo_ref, misfit_ref, part_ref, first_ref, second_ref, third_ref, send_sem, recv_sem):
-    x, y = position()
-    greet(x, y)
-    part_ref[...] = jnp.zeros_like(part_ref)
+    prepare(land_ref, fold_ref, state_ref)
+    legendre_body(d, wide_ref, state_ref, raw_ref)
+    power = power_body(d, raw_ref, turned_ref, sums_ref, shift_ref)
     for n in range(8):
-        part_ref[n, 0:4, :] = power_ref[4 * n : 4 * n + 4, :]
+        part_ref[n, 0:4, :] = power[4 * n : 4 * n + 4, :]
+        part_ref[n, 4:8, :] = jnp.zeros((4, 128), F32)
     for step in range(1, 8):
         to = (x + step) % 8
-        send(part_ref.at[to], first_ref.at[x], send_sem.at[0], recv_sem.at[0], device_at(to, y))
+        send(part_ref.at[to], first_ref.at[x], send_sem.at[2], recv_sem.at[2], device_at(to, y))
     first_ref[x] = part_ref[x]
-    drain(first_ref.at[pl.ds(0, 7)], recv_sem.at[0])
+    drain(first_ref.at[pl.ds(0, 7)], recv_sem.at[2])
     second_ref[y] = jnp.sum(first_ref[...], axis=0)
     for step in range(1, 16):
         to = (y + step) % 16
-        send(second_ref.at[y], second_ref.at[y], send_sem.at[1], recv_sem.at[1], device_at(x, to))
-    drain(second_ref.at[pl.ds(0, 15)], recv_sem.at[1])
+        send(second_ref.at[y], second_ref.at[y], send_sem.at[3], recv_sem.at[3], device_at(x, to))
+    drain(second_ref.at[pl.ds(0, 15)], recv_sem.at[3])
     third_ref[x] = jnp.sum(second_ref[...], axis=0)
     for step in range(1, 8):
         to = (x + step) % 8
-        send(third_ref.at[x], third_ref.at[x], send_sem.at[2], recv_sem.at[2], device_at(to, y))
-    drain(third_ref.at[pl.ds(0, 7)], recv_sem.at[2])
+        send(third_ref.at[x], third_ref.at[x], send_sem.at[4], recv_sem.at[4], device_at(to, y))
+    drain(third_ref.at[pl.ds(0, 7)], recv_sem.at[4])
     total = jnp.zeros((1, 1), F32)
     for n in range(8):
         pseudo = third_ref[n, 0:4, :]
@@ -403,42 +462,32 @@
         rel_error = (pseudo - model) / model
         total = total + jnp.sum(rel_error * rel_error, keepdims=True)
     misfit_ref[...] = total * (1.0 / LMAX)
-    drain(first_ref.at[pl.ds(0, 7)], send_sem.at[0])
-    drain(second_ref.at[pl.ds(0, 15)], send_sem.at[1])
-    drain(third_ref.at[pl.ds(0, 7)], send_sem.at[2])
-
-
-def legendre_kernel(got_ref, fold_ref, low_ref, high_ref, out_ref, coef_ref, gain_ref, state_ref, raw_ref, power_ref):
-    x, y = position()
-    d = order_block(x * 16 + y)
-    clear_gain(d, gain_ref)
-    tables_body(d, low_ref, high_ref, coef_ref, gain_ref)
-    prepare(got_ref, fold_ref, state_ref)
-    legendre_body(d, coef_ref, state_ref, raw_ref)
-    power_body(d, raw_ref, gain_ref, state_ref, power_ref)
-    out_ref[...] = power_ref[:, 0, :]
-
-
-LEGENDRE_SCRATCH = lambda: [
-    pltpu.VMEM((8, 544, 128), F32),
-    pltpu.VMEM((2, 4096 + 64, 128), F32),
-    pltpu.VMEM((2, 10, 8, 128), F32),
-    pltpu.VMEM((2, 2, 512 + 16, 8, 128), F32),
-    pltpu.VMEM((32, 8, 128), F32),
-]
+    drain(mid_ref.at[pl.ds(0, 7)], send_sem.at[0])
+    drain(land_ref.at[pl.ds(0, 15)], send_sem.at[1])
+    drain(first_ref.at[pl.ds(0, 7)], send_sem.at[2])
+    drain(second_ref.at[pl.ds(0, 15)], send_sem.at[3])
+    drain(third_ref.at[pl.ds(0, 7)], send_sem.at[4])
+
+
 VM = pl.BlockSpec(memory_space=pltpu.VMEM)
 SM = pl.BlockSpec(memory_space=pltpu.SMEM)
+HB = pl.BlockSpec(memory_space=pl.ANY)
 
 
 def on_device(pixels, block_ids, block_mask, model_cl):
     one, twist, two = dft_tables()
+    low, high = degree_tables()
+    spread = np.arange(128)[:, None] == 16 * (np.arange(1024) // 128) + np.arange(1024) % 16
+    tables = (one, twist, two, low, high, spread.astype(jnp.bfloat16), fold_matrix())
     dma = pltpu.SemaphoreType.DMA
-    received = pl.pallas_call(
-        fourier_kernel,
-        out_shape=jax.ShapeDtypeStruct((DEVICES, 128), F32),
-        in_specs=[VM] * 6 + [SM],
-        out_specs=VM,
-        scratch_shapes=[
+    pseudo_cl, misfit = pl.pallas_call(
+        everything,
+        out_shape=(jax.ShapeDtypeStruct((32, 128), F32), jax.ShapeDtypeStruct((1, 1), F32)),
+        in_specs=[VM] * 4 + [SM] + [HB] * 7,
+        out_specs=(VM, VM),
+        scratch_shapes=[pltpu.VMEM(table.shape, table.dtype) for table in tables]
+        + [
+            dma((7,)),
             pltpu.VMEM((16, BLOCK_PIX), F32),
             pltpu.VMEM((1, 16), jnp.int32),
             pltpu.VMEM((1, 16), jnp.int32),
@@ -446,37 +495,27 @@
             pltpu.VMEM((8, 16, 128), F32),
             pltpu.VMEM((16, 8, 128), F32),
             pltpu.VMEM((16, 8, 128), F32),
-            dma((3,)),
-            dma((3,)),
-            dma((2,)),
-            dma((2,)),
-        ],
-        compiler_params=pltpu.CompilerParams(collective_id=0, has_side_effects=True),
-    )(pixels, block_ids.reshape(1, 16), block_mask.reshape(1, 16), one, twist, two, half_logs())
-    low, high = degree_tables()
-    power = pl.pallas_call(
-        legendre_kernel,
-        out_shape=jax.ShapeDtypeStruct((32, 128), F32),
-        in_specs=[VM] * 4,
-        out_specs=VM,
-        scratch_shapes=LEGENDRE_SCRATCH(),
-        compiler_params=pltpu.CompilerParams(vmem_limit_bytes=40 * 1024 * 1024),
-    )(received, fold_matrix(), low, high)
-    pseudo_cl, misfit = pl.pallas_call(
-        reduce_kernel,
-        out_shape=(jax.ShapeDtypeStruct((32, 128), F32), jax.ShapeDtypeStruct((1, 1), F32)),
-        in_specs=[VM] * 2,
-        out_specs=(VM, VM),
-        scratch_shapes=[
+            pltpu.VMEM((ROWS, 128), F32),
+            pltpu.VMEM((ROWS, 128), F32),
+            pltpu.VMEM((8, ROWS, 128), F32),
+            pltpu.VMEM((TILES, 16, 128), F32),
+            pltpu.VMEM((2, 10, 8, 128), F32),
+            pltpu.VMEM((2, 528, 8, 128), F32),
+            pltpu.VMEM((40, 128), F32),
+            pltpu.VMEM((72, 128), F32),
             pltpu.VMEM((8, 8, 128), F32),
             pltpu.VMEM((8, 8, 128), F32),
             pltpu.VMEM((16, 8, 128), F32),
             pltpu.VMEM((8, 8, 128), F32),
             dma((3,)),
             dma((3,)),
+            dma((5,)),
+            dma((5,)),
         ],
-        compiler_params=pltpu.CompilerParams(collective_id=1, has_side_effects=True),
-    )(power, model_cl.reshape(32, 128))
+        compiler_params=pltpu.CompilerParams(
+            collective_id=0, has_side_effects=True, vmem_limit_bytes=56 * 1024 * 1024
+        ),
+    )(pixels, block_ids.reshape(1, 16), block_mask.reshape(1, 16), model_cl.reshape(32, 128), half_logs(), *tables)
     return pseudo_cl.reshape(LMAX), misfit.reshape(())
 
 

time: 80 us -> 56.8 us (0.71)
  Pallas kernels: 72.5 us -> 52.8 us
  local copies, waits for them, and re-layouts: 4.62 us -> 1.32 us
    pallas_call x3 -> x1, Pallas kernels: 72.5 us -> 52.8 us  [on_device(): pl.pallas_call(everything, out_shape=(jax.ShapeDtypeStruct((32, 128), F32...]
    unnamed x11 -> x1, local copies, waits for them, and re-layouts: 4.62 us -> 1.32 us
where the time goes in v2:
time: 56.8 us; the launch traced here: 56.5 us
  Pallas kernels  52.8 us (93%)
  between operations  2.4 us (4%)
  local copies, waits for them, and re-layouts  1.32 us (2%)
    pallas_call x1, Pallas kernels, on_device(): pl.pallas_call(everything, out_shape=(jax.ShapeDtypeStruct((32, 128), F32...  52.8 us
    unnamed x1, local copies, waits for them, and re-layouts  1.32 us

profile of v2, /device:TPU:1, one launch (start us, length us, event | category | flops | bytes accessed | tf_op | source)
XLA Modules:
  0.0 56.5 jit_solution(6602569551433036809)
XLA Ops:
  0.6 52.8 %shard_map.131 = (f32[32,128]{1,0:T(8,128)}, f32[1,1]{1,0:T(1,128)}) custom-call(f32[16,1024]{1,0:T(8,128)} %own_ref.1, s32[1,16]{1,0:T(1,128)} %bitcast.7, s32[1,16]{1,0:T(1,128)} %bitcast.8, f32[32,128]{1,0:T(8,128)} %bitcast.5, f32[256]{0:T(256)} %constant.16.clone.logs_ref, f32[128,64]{1,0:T(8,128)} %constant.17.clone.one_hbm, ...), custom_call_target="tpu_custom_call" | custom-call | tf_op jit(solution)/shard_map/pallas_call | solution.py:483
  53.4 1.3 %copy.16 = f32[4096]{0:T(1024)} copy(f32[4096]{0:T(1024)} %bitcast.6) | data formatting | bytes 32768

commit v3 on v2

--- a/solution.py
+++ b/solution.py
@@ -21,7 +21,7 @@
 BF16 = jnp.bfloat16
 ROWS = 544
 TILES = 33
-POWER_UNROLL = 3
+CUTS = (20, 75)
 
 
 def dft_tables():
@@ -101,42 +101,57 @@
 EQUATOR_ROW = 4
 
 
-def fourier_body(owner, own_ref, own_ids_ref, own_mask_ref, got_ref, got_ids_ref, got_mask_ref, one_ref, twist_ref, two_ref, logs_ref, out_ref):
-    slot = lax.broadcasted_iota(jnp.int32, (16, 16), 0) + owner * 16
-    pick_own = jnp.where(own_ids_ref[...] == slot, own_mask_ref[...], 0).astype(F32)
-    pick_got = jnp.where(got_ids_ref[...] == slot, got_mask_ref[...], 0).astype(F32)
-    rows = jnp.dot(pick_own, own_ref[...], precision=HIGHEST, preferred_element_type=F32) + jnp.dot(
-        pick_got, got_ref[...], precision=HIGHEST, preferred_element_type=F32
-    )
+def fourier_body(pair, ids_ref, mask_ref, own_ref, one_ref, twist_ref, two_ref, logs_ref, out_ref):
+    row = lax.broadcasted_iota(jnp.int32, (32, 16), 0)
+    slot = (pair + 64 * (row // 16)) * 16 + row % 16
+    pick = jnp.where(ids_ref[...] == slot, mask_ref[...], 0).astype(F32)
+    rows = jnp.dot(pick, own_ref[...], precision=HIGHEST, preferred_element_type=F32)
     folded = jnp.concatenate(
         [
-            jnp.concatenate([rows[8 * c : 8 * c + 8, 128 * p : 128 * p + 128] for p in range(8)], axis=0)
-            for c in range(2)
+            jnp.concatenate([rows[8 * n : 8 * n + 8, 128 * p : 128 * p + 128] for p in range(8)], axis=0)
+            for n in range(4)
         ],
         axis=1,
     )
     first = jnp.dot(one_ref[...], folded, precision=HIGHEST, preferred_element_type=F32)
     k1 = lax.broadcasted_iota(jnp.int32, (64, 64), 1)
-    row = lax.broadcasted_iota(jnp.int32, (64, 64), 0)
-    orders = (k1 + 64 * jnp.where(row < 32, row, 95 - row)).astype(F32)
-    outs = []
+    upper = lax.broadcasted_iota(jnp.int32, (64, 64), 0)
+    orders = (k1 + 64 * jnp.where(upper < 32, upper, 95 - upper)).astype(F32)
+    outs = [[None, None], [None, None]]
     for c in range(2):
-        re, im = first[0:64, 128 * c : 128 * c + 128], first[64:128, 128 * c : 128 * c + 128]
         cos, sin = twist_ref[c, 0], twist_ref[c, 1]
-        turned = jnp.concatenate([re * cos + im * sin, im * cos - re * sin], axis=1)
+        turned = []
+        for band in range(2):
+            lanes = slice(128 * (2 * band + c), 128 * (2 * band + c) + 128)
+            re, im = first[0:64, lanes], first[64:128, lanes]
+            turned.append(jnp.concatenate([re * cos + im * sin, im * cos - re * sin], axis=1))
         spec = lax.dot_general(
-            two_ref[c], turned, (((1,), (1,)), ((), ())), precision=HIGHEST, preferred_element_type=F32
+            two_ref[c],
+            jnp.concatenate(turned, axis=0),
+            (((1,), (1,)), ((), ())),
+            precision=HIGHEST,
+            preferred_element_type=F32,
         )
-        seed = jnp.exp(orders * logs_ref[owner * 2 + c])
-        outs.append((spec[0:64] * seed, spec[64:128] * seed))
-    for j in range(4):
-        pieces = []
-        for ri in range(2):
-            for half in range(2):
-                jj = j if half == 0 else 3 - j
-                for c in range(2):
-                    pieces.append(outs[c][ri][32 * half : 32 * half + 32, 16 * jj : 16 * jj + 16])
-        out_ref[2 * j : 2 * j + 2] = jnp.concatenate(pieces, axis=1).reshape(2, 16, 128)
+        for band in range(2):
+            seed = jnp.exp(orders * logs_ref[2 * (pair + 64 * band) + c])
+            lanes = slice(64 * band, 64 * band + 64)
+            outs[band][c] = (spec[0:64, lanes] * seed, spec[64:128, lanes] * seed)
+    for band in range(2):
+        for j in range(4):
+            pieces = []
+            for ri in range(2):
+                for half in range(2):
+                    jj = j if half == 0 else 3 - j
+                    for c in range(2):
+                        pieces.append(outs[band][c][ri][32 * half : 32 * half + 32, 16 * jj : 16 * jj + 16])
+            joined = jnp.concatenate(pieces, axis=1)
+            for n in range(2):
+                out_ref[2 * j + n, band] = joined[16 * n : 16 * n + 16]
+
+
+def two_pieces(value):
+    high = value.astype(BF16)
+    return jnp.concatenate([high, (value - high.astype(F32)).astype(BF16)], axis=1)
 
 
 def pieces_of(value):
@@ -146,18 +161,8 @@
     return high, middle, (rest - middle.astype(F32)).astype(BF16)
 
 
-def lane_groups():
-    row = lax.broadcasted_iota(jnp.int32, (16, 128), 0)
-    lane = lax.broadcasted_iota(jnp.int32, (16, 128), 1)
-    return jnp.where(lane % 16 == row, 1.0, 0.0).astype(BF16)
-
-
-def grouped(groups, pieces):
-    total = None
-    for piece in pieces:
-        part = lax.dot_general(groups, piece, (((1,), (1,)), ((), ())), preferred_element_type=F32)
-        total = part if total is None else total + part
-    return total
+def blocks_before(d):
+    return 512 - 16 * (d // 8)
 
 
 def compact_tables(d, low_ref, high_ref, coef_ref, gain_ref):
@@ -165,9 +170,11 @@
     lane = lax.broadcasted_iota(jnp.int32, (8, 128), 1)
     order = lane % 16
     offset = 8 * row + lane // 16
+    coef_ref[...] = jnp.zeros((ROWS, 128), F32)
+    gain_ref[...] = jnp.zeros((ROWS, 128), F32)
     for half in range(2):
         first = first_order(d, half)
-        start = 0 if half == 0 else 512 - 2 * d
+        start = 0 if half == 0 else blocks_before(d)
 
         def one(k, carry):
             low = low_ref[pl.ds(pl.multiple_of(8 * k, 8), 8), :]
@@ -199,17 +206,22 @@
             wide_ref[step, at, :] = total[:, 128 * step : 128 * step + 128]
 
 
-def spread_gain(gain_ref, turned_ref):
-    groups = lane_groups()
-    row = lax.broadcasted_iota(jnp.int32, (8, 128), 0)
-    lane = lax.broadcasted_iota(jnp.int32, (8, 128), 1)
-    same = lane // 16 == row
+def spread_gain(gain_ref, spread_ref, wide_ref, gains_ref):
+    spread = jnp.concatenate([spread_ref[...]] * 2, axis=0)
+    for chunk in range(4):
+        start = ROWS // 4 * chunk
+        total = jnp.dot(two_pieces(gain_ref[pl.ds(start, ROWS // 4), :]), spread, preferred_element_type=F32)
+        for step in range(8):
+            wide_ref[pl.ds(8 * start + step, ROWS // 4, stride=8), :] = total[:, 128 * step : 128 * step + 128]
+    quarter = lax.broadcasted_iota(jnp.int32, (8, 128), 1) // 16 % 4
 
     def one(tile, carry):
-        rows = [
-            jnp.where(same, jnp.broadcast_to(gain_ref[pl.ds(16 * tile + n, 1), :], (8, 128)), 0.0) for n in range(16)
-        ]
-        turned_ref[tile] = grouped(groups, pieces_of(jnp.concatenate(rows, axis=0)))
+        for n in range(4):
+            packed = None
+            for q in range(4):
+                rows = wide_ref[pl.ds(pl.multiple_of(128 * tile + 32 * q + 8 * n, 8), 8), :]
+                packed = rows if packed is None else jnp.where(quarter == q, rows, packed)
+            gains_ref[4 * tile + n] = packed
         return carry
 
     lax.fori_loop(0, TILES, one, 0)
@@ -254,93 +266,137 @@
     return 16 * d if half == 0 else 4080 - 16 * d
 
 
-UNROLL = 8
-
-
-def legendre_body(d, coef_ref, state_ref, raw_ref):
+def first_order(d, half):
+    return 16 * d if half == 0 else 4080 - 16 * d
+
+
+def latitudes():
     row = lax.broadcasted_iota(jnp.int32, (8, 128), 0)
     lane = lax.broadcasted_iota(jnp.int32, (8, 128), 1)
-    order = lane % 16
-    masks = ((row & 1) == 0, (row & 2) == 0, (row & 4) == 0)
     lats = []
     for v in range(2):
         u = 32 * v + 8 * (lane // 32) + row
         q = 2 * u + jnp.where((lane % 32) < 16, 2, 1)
         lats.append(q.astype(F32) * (2.0 / (3.0 * NSIDE)))
-
-    def merge(level, first, second):
-        mask = masks[level]
-        shift = 8 - (1 << level)
-        return jnp.where(mask, first, second) + pltpu.roll(jnp.where(mask, second, first), shift, 0)
-
-    def eight(base, weights, state, seeded, k):
-        a0, a1, b0, b1 = state
-        stack = {}
-        for step in range(8):
-            coef = jnp.broadcast_to(coef_ref[step, pl.ds(base + k, 1), :], (8, 128))
-            n0 = (coef * lats[0]) * a0 - b0
-            n1 = (coef * lats[1]) * a1 - b1
-            if seeded is not None:
-                start = order == (seeded * 8 + step)
-                n0 = jnp.where(start, 1.0, n0)
-                n1 = jnp.where(start, 1.0, n1)
-            a0, a1, b0, b1 = n0, n1, a0, a1
-            p = step % 2
+    return lats
+
+
+def value_of(order, fresh, step):
+    return jnp.where(order == step, fresh, 0.0)
+
+
+def recur(d, coef_ref, values_ref, low, top, state):
+    order = lax.broadcasted_iota(jnp.int32, (8, 128), 1) % 16
+    lats = latitudes()
+    restart = blocks_before(d) // 4
+
+    def quad(n, state):
+        fresh = jnp.where((n == 0) | (n == restart), 1.0, 0.0)
+        a0, a1, b0, b1 = [value * (1.0 - fresh) for value in state]
+        for step in range(0, 32, 2):
+            block = 4 * n + step // 8
+            now, later = [
+                jnp.broadcast_to(coef_ref[(step + k) % 8, pl.ds(block, 1), :], (8, 128)) for k in range(2)
+            ]
+            ones = [value_of(order, fresh, step + k) for k in range(2)] if step < 16 else None
+            fresh_pair = []
+            for v, (one_back, two_back) in enumerate(((a0, b0), (a1, b1))):
+                c0, c1 = now * lats[v], later * lats[v]
+                if ones is not None:
+                    two_back = two_back - ones[0]
+                rest = c1 * two_back
+                if ones is not None:
+                    rest = rest - ones[1]
+                first = c0 * one_back - two_back
+                second = (c1 * c0 - 1.0) * one_back - rest
+                values_ref[block, v, pl.ds(step % 8, 8, stride=8), :] = first
+                values_ref[block, v, pl.ds(step % 8 + 1, 8, stride=8), :] = second
+                fresh_pair.append((second, first))
+            (a0, b0), (a1, b1) = fresh_pair
+        return (a0, a1, b0, b1)
+
+    return lax.fori_loop(low, top, quad, state)
+
+
+def widen_weights(state_ref, weights_ref):
+    even_row = (lax.broadcasted_iota(jnp.int32, (8, 128), 0) & 1) == 0
+    for half in range(2):
+        for v in range(2):
             for ri in range(2):
-                term = n0 * weights[4 * p + 2 * ri] + n1 * weights[4 * p + 2 * ri + 1]
-                level, idx = 0, step
-                while idx % 2 == 1:
-                    term = merge(level, stack.pop((ri, level)), term)
-                    level, idx = level + 1, idx // 2
-                stack[(ri, level)] = term
-        for ri in range(2):
-            raw_ref[ri, base + k] = stack[(ri, 3)] + weights[8 + ri]
-        return (a0, a1, b0, b1)
-
-    for half in range(2):
-        first = first_order(d, half)
-        base = 0 if half == 0 else 512 - 2 * d
-        weights = [state_ref[half, n] for n in range(10)]
-        zero = jnp.zeros((8, 128), F32)
-        state = (zero, zero, zero, zero)
-        for k in range(2):
-            state = eight(base, weights, state, k, k)
-        def many(n, state):
-            for k in range(UNROLL):
-                state = eight(base, weights, state, None, UNROLL * n + k + 2)
-            return state
-
-        lax.fori_loop(0, ((4096 - first) // 8 - 2 + UNROLL - 1) // UNROLL, many, state)
-
-
-def power_body(d, raw_ref, turned_ref, rows_ref, shift_ref):
-    groups = lane_groups()
-
+                even, odd = state_ref[half, 2 * ri + v], state_ref[half, 4 + 2 * ri + v]
+                for s in range(8):
+                    weights_ref[half, v, s, ri] = jnp.where(
+                        even_row,
+                        jnp.broadcast_to(even[s : s + 1], (8, 128)),
+                        jnp.broadcast_to(odd[s : s + 1], (8, 128)),
+                    )
+
+
+def contract(d, values_ref, weights_ref, state_ref, gains_ref, squares_ref, tile):
+    lane = lax.broadcasted_iota(jnp.int32, (8, 128), 1)
+    masks = {shift: (lane & shift) == 0 for shift in (16, 32, 64)}
+
+    def merge(shift, first, second):
+        mask = masks[shift]
+        return jnp.where(mask, first, second) + pltpu.roll(jnp.where(mask, second, first), 128 - shift, 1)
+
+    half = jnp.where(16 * tile >= blocks_before(d), 1, 0)
+    for n in range(4):
+        blocks = [16 * tile + n + 4 * q for q in range(4)]
+        sums = [[state_ref[half, 8 + ri]] * 4 for ri in range(2)]
+        for v in range(2):
+            for s in range(8):
+                weights = [weights_ref[half, v, s, ri] for ri in range(2)]
+                for q in range(4):
+                    value = values_ref[blocks[q], v, 8 * s : 8 * s + 8, :]
+                    for ri in range(2):
+                        sums[ri][q] = sums[ri][q] + value * weights[ri]
+        parts = [
+            merge(32, merge(16, sums[ri][0], sums[ri][1]), merge(16, sums[ri][2], sums[ri][3])) for ri in range(2)
+        ]
+        packed = merge(64, parts[0], parts[1])
+        squares_ref[4 * tile + n] = packed * packed * gains_ref[4 * tile + n]
+
+
+def power_body(d, values_ref, weights_ref, state_ref, gains_ref, squares_ref, columns_ref, turned_ref, shift_ref):
     def one(tile, carry):
-        total = None
-        for ri in range(2):
-            value = raw_ref[ri, pl.ds(pl.multiple_of(16 * tile, 16), 16)].reshape(128, 128)
-            value = grouped(groups, pieces_of(value))
-            total = value * value if total is None else total + value * value
-        rows_ref[pl.ds(tile, 1), :] = jnp.sum(total * turned_ref[tile], axis=0, keepdims=True)
+        contract(d, values_ref, weights_ref, state_ref, gains_ref, squares_ref, tile)
         return carry
 
-    def several(n, carry):
-        for k in range(POWER_UNROLL):
-            one(POWER_UNROLL * n + k, carry)
+    def many(k, carry):
+        for n in range(3):
+            one(3 * k + n, carry)
         return carry
 
-    lax.fori_loop(0, TILES // POWER_UNROLL, several, 0)
-    bound = 4096 - 16 * d
+    lax.fori_loop(0, TILES // 3, many, 0)
+    row = lax.broadcasted_iota(jnp.int32, (256, 128), 0)
+    column = lax.broadcasted_iota(jnp.int32, (256, 128), 1)
+    quarters = jnp.where(row // 16 % 4 == column % 4, 1.0, 0.0).astype(BF16)
+    columns_ref[...] = jnp.dot(
+        two_pieces(squares_ref[...].reshape(32 * TILES, 128)), quarters, preferred_element_type=F32
+    )
+    lane = lax.broadcasted_iota(jnp.int32, (32, 128), 1)
+    tables = [jnp.zeros((32, 128), F32), jnp.zeros((32, 128), F32)]
+    for tile in range(TILES):
+        tables[tile // 32] = jnp.where(
+            lane // 4 == tile % 32, columns_ref[32 * tile : 32 * tile + 32, :], tables[tile // 32]
+        )
+    for n in range(2):
+        table = jnp.concatenate([tables[n], jnp.zeros((96, 128), F32)], axis=0)
+        turned_ref[128 * n : 128 * n + 128, :] = jnp.transpose(table)
+    rows = turned_ref[pl.ds(0, 40, stride=4), :]
+    for q in range(1, 4):
+        rows = rows + pltpu.roll(turned_ref[pl.ds(q, 40, stride=4), :], 32 * q, 1)
+    begin = 8 * blocks_before(d)
     step = 128 * lax.broadcasted_iota(jnp.int32, (40, 128), 0) + lax.broadcasted_iota(jnp.int32, (40, 128), 1)
-    rows = rows_ref[...]
     shift_ref[0:32, :] = jnp.zeros((32, 128), F32)
-    shift_ref[32:72, :] = pltpu.roll(jnp.where(step < bound, rows, 0.0), 16 * (d % 8), 1)
-    later = pltpu.roll(jnp.where((step >= bound) & (step < 4112), rows, 0.0), 112, 1)
+    shift_ref[32:72, :] = pltpu.roll(jnp.where(step < 4096 - 16 * d, rows, 0.0), 16 * (d % 8), 1)
+    back = 16 + 16 * (d % 8)
+    later = pltpu.roll(jnp.where((step >= begin) & (step < begin + 16 * d + 16), rows, 0.0), 128 - back, 1)
     lane = lax.broadcasted_iota(jnp.int32, (32, 128), 1)
     near = shift_ref[pl.ds(32 - d // 8, 32), :]
     far = shift_ref[pl.ds(31 - d // 8, 32), :]
-    return jnp.where(lane >= 16 * (d % 8), near, far) + jnp.where(lane < 112, later[0:32], later[1:33])
+    return jnp.where(lane >= 16 * (d % 8), near, far) + jnp.where(lane < 128 - back, later[0:32], later[1:33])
 
 
 def position():
@@ -362,7 +418,7 @@
         pl.semaphore_signal(barrier, inc=1, device_id=device_at((x + step) % 8, y), device_id_type=MESH)
     for step in range(1, 16):
         pl.semaphore_signal(barrier, inc=1, device_id=device_at(x, (y + step) % 16), device_id_type=MESH)
-    pl.semaphore_wait(barrier, 22)
+    return barrier
 
 
 def send(source, target, send_sem, recv_sem, device):
@@ -378,64 +434,63 @@
 
 
 def everything(
-    own_ref, own_ids_ref, own_mask_ref, model_ref, logs_ref,
-    one_hbm, twist_hbm, two_hbm, low_hbm, high_hbm, spread_hbm, fold_hbm,
+    pixels_hbm, ids_hbm, mask_hbm, model_hbm, logs_hbm, one_hbm, twist_hbm, two_hbm, low_hbm, high_hbm, spread_hbm, fold_hbm,
     pseudo_ref, misfit_ref,
-    one_ref, twist_ref, two_ref, low_ref, high_ref, spread_ref, fold_ref, local_sem,
-    got_ref, got_ids_ref, got_mask_ref, rows_ref, mid_ref, again_ref, land_ref,
-    coef_ref, gain_ref, wide_ref, turned_ref, state_ref, raw_ref, sums_ref, shift_ref,
-    part_ref, first_ref, second_ref, third_ref,
-    pair_send, pair_recv, send_sem, recv_sem,
+    own_ref, ids_ref, mask_ref, model_ref, logs_ref, one_ref, twist_ref, two_ref, low_ref, high_ref, spread_ref, fold_ref,
+    local_sem,
+    rows_ref, mid_ref, joined_ref, again_ref, land_ref,
+    coef_ref, gain_ref, wide_ref, broad_ref, gains_ref, state_ref, weights_ref, values_ref, squares_ref,
+    columns_ref, turned_ref, shift_ref, part_ref, first_ref, second_ref, third_ref, send_sem, recv_sem,
 ):
     x, y = position()
     d = order_block(x * 16 + y)
-    owner = (x // 4) * 64 + y * 4 + x % 4
+    barrier = greet(x, y)
     loads = [
         pltpu.make_async_copy(source, target, local_sem.at[n])
         for n, (source, target) in enumerate(
             (
-                (one_hbm, one_ref), (twist_hbm, twist_ref), (two_hbm, two_ref), (low_hbm, low_ref),
-                (high_hbm, high_ref), (spread_hbm, spread_ref), (fold_hbm, fold_ref),
+                (low_hbm, low_ref), (high_hbm, high_ref), (spread_hbm, spread_ref), (one_hbm, one_ref),
+                (twist_hbm, twist_ref), (two_hbm, two_ref), (fold_hbm, fold_ref), (pixels_hbm, own_ref),
+                (ids_hbm, ids_ref), (mask_hbm, mask_ref), (model_hbm, model_ref), (logs_hbm, logs_ref),
             )
         )
     ]
-    greet(x, y)
     for copy in loads:
         copy.start()
-    partner = device_at((x + 4) % 8, y)
-    pair = [
-        send(source, target, pair_send.at[n], pair_recv.at[n], partner)
-        for n, (source, target) in enumerate(
-            ((own_ref, got_ref), (own_ids_ref, got_ids_ref), (own_mask_ref, got_mask_ref))
-        )
-    ]
-    for copy in loads:
+    for copy in loads[0:3]:
         copy.wait()
     compact_tables(d, low_ref, high_ref, coef_ref, gain_ref)
-    for copy in pair:
+    spread_coef(coef_ref, spread_ref, wide_ref)
+    spread_gain(gain_ref, spread_ref, broad_ref, gains_ref)
+    zero = jnp.zeros((8, 128), F32)
+    state = recur(d, wide_ref, values_ref, 0, CUTS[0], (zero, zero, zero, zero))
+    for copy in loads[3:]:
         copy.wait()
-    fourier_body(
-        owner, own_ref, own_ids_ref, own_mask_ref, got_ref, got_ids_ref, got_mask_ref,
-        one_ref, twist_ref, two_ref, logs_ref, rows_ref,
-    )
+    fourier_body(y * 4 + x % 4, ids_ref, mask_ref, own_ref, one_ref, twist_ref, two_ref, logs_ref, rows_ref)
+    pl.semaphore_wait(barrier, 22)
     for step in range(1, 8):
         to = (x + step) % 8
         send(rows_ref.at[to], mid_ref.at[x], send_sem.at[0], recv_sem.at[0], device_at(to, y))
     mid_ref[x] = rows_ref[x]
-    spread_coef(coef_ref, spread_ref, wide_ref)
+    state = recur(d, wide_ref, values_ref, CUTS[0], CUTS[1], state)
     drain(mid_ref.at[pl.ds(0, 7)], recv_sem.at[0])
-    every = mid_ref[...]
+    for band in range(2):
+        for n in range(4):
+            at = 64 * band + 16 * n
+            joined_ref[at : at + 16, :] = mid_ref[n, band] + mid_ref[4 + n, band]
     for to in range(16):
-        again_ref[to] = jnp.concatenate([every[n, to : to + 1, :] for n in range(8)], axis=0)
+        again_ref[to] = joined_ref[pl.ds(to, 8, stride=16), :]
     for step in range(1, 16):
         to = (y + step) % 16
         send(again_ref.at[to], land_ref.at[y], send_sem.at[1], recv_sem.at[1], device_at(x, to))
     land_ref[y] = again_ref[y]
-    spread_gain(gain_ref, turned_ref)
+    recur(d, wide_ref, values_ref, CUTS[1], 4 * TILES, state)
     drain(land_ref.at[pl.ds(0, 15)], recv_sem.at[1])
     prepare(land_ref, fold_ref, state_ref)
-    legendre_body(d, wide_ref, state_ref, raw_ref)
-    power = power_body(d, raw_ref, turned_ref, sums_ref, shift_ref)
+    widen_weights(state_ref, weights_ref)
+    power = power_body(
+        d, values_ref, weights_ref, state_ref, gains_ref, squares_ref, columns_ref, turned_ref, shift_ref
+    )
     for n in range(8):
         part_ref[n, 0:4, :] = power[4 * n : 4 * n + 4, :]
         part_ref[n, 4:8, :] = jnp.zeros((4, 128), F32)
@@ -470,7 +525,6 @@
 
 
 VM = pl.BlockSpec(memory_space=pltpu.VMEM)
-SM = pl.BlockSpec(memory_space=pltpu.SMEM)
 HB = pl.BlockSpec(memory_space=pl.ANY)
 
 
@@ -483,37 +537,44 @@
     pseudo_cl, misfit = pl.pallas_call(
         everything,
         out_shape=(jax.ShapeDtypeStruct((32, 128), F32), jax.ShapeDtypeStruct((1, 1), F32)),
-        in_specs=[VM] * 4 + [SM] + [HB] * 7,
+        in_specs=[HB] * 12,
         out_specs=(VM, VM),
-        scratch_shapes=[pltpu.VMEM(table.shape, table.dtype) for table in tables]
-        + [
-            dma((7,)),
+        scratch_shapes=[
             pltpu.VMEM((16, BLOCK_PIX), F32),
             pltpu.VMEM((1, 16), jnp.int32),
             pltpu.VMEM((1, 16), jnp.int32),
-            pltpu.VMEM((8, 16, 128), F32),
-            pltpu.VMEM((8, 16, 128), F32),
+            pltpu.VMEM((32, 128), F32),
+            pltpu.SMEM((CYCLES,), F32),
+        ]
+        + [pltpu.VMEM(table.shape, table.dtype) for table in tables]
+        + [
+            dma((12,)),
+            pltpu.VMEM((8, 2, 16, 128), F32),
+            pltpu.VMEM((8, 2, 16, 128), F32),
+            pltpu.VMEM((128, 128), F32),
             pltpu.VMEM((16, 8, 128), F32),
             pltpu.VMEM((16, 8, 128), F32),
             pltpu.VMEM((ROWS, 128), F32),
             pltpu.VMEM((ROWS, 128), F32),
             pltpu.VMEM((8, ROWS, 128), F32),
-            pltpu.VMEM((TILES, 16, 128), F32),
+            pltpu.VMEM((8 * ROWS, 128), F32),
+            pltpu.VMEM((4 * TILES, 8, 128), F32),
             pltpu.VMEM((2, 10, 8, 128), F32),
-            pltpu.VMEM((2, 528, 8, 128), F32),
-            pltpu.VMEM((40, 128), F32),
+            pltpu.VMEM((2, 2, 8, 2, 8, 128), F32),
+            pltpu.VMEM((16 * TILES, 2, 64, 128), F32),
+            pltpu.VMEM((4 * TILES, 8, 128), F32),
+            pltpu.VMEM((32 * TILES, 128), F32),
+            pltpu.VMEM((256, 128), F32),
             pltpu.VMEM((72, 128), F32),
             pltpu.VMEM((8, 8, 128), F32),
             pltpu.VMEM((8, 8, 128), F32),
             pltpu.VMEM((16, 8, 128), F32),
             pltpu.VMEM((8, 8, 128), F32),
-            dma((3,)),
-            dma((3,)),
             dma((5,)),
             dma((5,)),
         ],
         compiler_params=pltpu.CompilerParams(
-            collective_id=0, has_side_effects=True, vmem_limit_bytes=56 * 1024 * 1024
+            collective_id=0, has_side_effects=True, vmem_limit_bytes=60 * 1024 * 1024
         ),
     )(pixels, block_ids.reshape(1, 16), block_mask.reshape(1, 16), model_cl.reshape(32, 128), half_logs(), *tables)
     return pseudo_cl.reshape(LMAX), misfit.reshape(())

time: 56.8 us -> 45.6 us (0.80)
  Pallas kernels: 52.8 us -> 41.7 us
    pallas_call x1, Pallas kernels: 52.8 us -> 41.7 us  [on_device(): pl.pallas_call(everything, out_shape=(jax.ShapeDtypeStruct((32, 128), F32...]
where the time goes in v3:
time: 45.6 us; the launch traced here: 45.4 us
  Pallas kernels  41.7 us (91%)
  between operations  2.4 us (5%)
  local copies, waits for them, and re-layouts  1.32 us (3%)
    pallas_call x1, Pallas kernels, on_device(): pl.pallas_call(everything, out_shape=(jax.ShapeDtypeStruct((32, 128), F32...  41.7 us
    unnamed x1, local copies, waits for them, and re-layouts  1.32 us

profile of v3, /device:TPU:1, one launch (start us, length us, event | category | flops | bytes accessed | tf_op | source)
XLA Modules:
  0.0 45.4 jit_solution(15694562867848676611)
XLA Ops:
  0.6 41.7 %shard_map.131 = (f32[32,128]{1,0:T(8,128)}, f32[1,1]{1,0:T(1,128)}) custom-call(f32[16,1024]{1,0:T(8,128)} %pixels_hbm.1, s32[1,16]{1,0:T(1,128)} %bitcast.7, s32[1,16]{1,0:T(1,128)} %bitcast.8, f32[32,128]{1,0:T(8,128)} %bitcast.5, f32[256]{0:T(256)} %constant.16.clone.logs_hbm, f32[128,64]{1,0:T(8,128)} %constant.17.clone.one_hbm, ...), custom_call_target="tpu_custom_call" | custom-call | tf_op jit(solution)/shard_map/pallas_call | solution.py:537
  42.3 1.3 %copy.16 = f32[4096]{0:T(1024)} copy(f32[4096]{0:T(1024)} %bitcast.6) | data formatting | bytes 32768

commit v4 on v3

--- a/solution.py
+++ b/solution.py
@@ -21,7 +21,7 @@
 BF16 = jnp.bfloat16
 ROWS = 544
 TILES = 33
-CUTS = (20, 75)
+CUT = 55
 
 
 def dft_tables():
@@ -224,7 +224,12 @@
             gains_ref[4 * tile + n] = packed
         return carry
 
-    lax.fori_loop(0, TILES, one, 0)
+    def many(k, carry):
+        for n in range(3):
+            one(3 * k + n, carry)
+        return carry
+
+    lax.fori_loop(0, TILES // 3, many, 0)
 
 
 def prepare(got_ref, fold_ref, state_ref):
@@ -440,7 +445,7 @@
     local_sem,
     rows_ref, mid_ref, joined_ref, again_ref, land_ref,
     coef_ref, gain_ref, wide_ref, broad_ref, gains_ref, state_ref, weights_ref, values_ref, squares_ref,
-    columns_ref, turned_ref, shift_ref, part_ref, first_ref, second_ref, third_ref, send_sem, recv_sem,
+    columns_ref, turned_ref, shift_ref, part_ref, first_ref, second_ref, send_sem, recv_sem,
 ):
     x, y = position()
     d = order_block(x * 16 + y)
@@ -462,8 +467,6 @@
     compact_tables(d, low_ref, high_ref, coef_ref, gain_ref)
     spread_coef(coef_ref, spread_ref, wide_ref)
     spread_gain(gain_ref, spread_ref, broad_ref, gains_ref)
-    zero = jnp.zeros((8, 128), F32)
-    state = recur(d, wide_ref, values_ref, 0, CUTS[0], (zero, zero, zero, zero))
     for copy in loads[3:]:
         copy.wait()
     fourier_body(y * 4 + x % 4, ids_ref, mask_ref, own_ref, one_ref, twist_ref, two_ref, logs_ref, rows_ref)
@@ -472,7 +475,8 @@
         to = (x + step) % 8
         send(rows_ref.at[to], mid_ref.at[x], send_sem.at[0], recv_sem.at[0], device_at(to, y))
     mid_ref[x] = rows_ref[x]
-    state = recur(d, wide_ref, values_ref, CUTS[0], CUTS[1], state)
+    zero = jnp.zeros((8, 128), F32)
+    state = recur(d, wide_ref, values_ref, 0, CUT, (zero, zero, zero, zero))
     drain(mid_ref.at[pl.ds(0, 7)], recv_sem.at[0])
     for band in range(2):
         for n in range(4):
@@ -484,44 +488,34 @@
         to = (y + step) % 16
         send(again_ref.at[to], land_ref.at[y], send_sem.at[1], recv_sem.at[1], device_at(x, to))
     land_ref[y] = again_ref[y]
-    recur(d, wide_ref, values_ref, CUTS[1], 4 * TILES, state)
+    recur(d, wide_ref, values_ref, CUT, 4 * TILES, state)
     drain(land_ref.at[pl.ds(0, 15)], recv_sem.at[1])
     prepare(land_ref, fold_ref, state_ref)
     widen_weights(state_ref, weights_ref)
     power = power_body(
         d, values_ref, weights_ref, state_ref, gains_ref, squares_ref, columns_ref, turned_ref, shift_ref
     )
-    for n in range(8):
-        part_ref[n, 0:4, :] = power[4 * n : 4 * n + 4, :]
-        part_ref[n, 4:8, :] = jnp.zeros((4, 128), F32)
+    part_ref[...] = power
+    first_ref[x] = power
     for step in range(1, 8):
         to = (x + step) % 8
-        send(part_ref.at[to], first_ref.at[x], send_sem.at[2], recv_sem.at[2], device_at(to, y))
-    first_ref[x] = part_ref[x]
+        send(part_ref, first_ref.at[x], send_sem.at[2], recv_sem.at[2], device_at(to, y))
     drain(first_ref.at[pl.ds(0, 7)], recv_sem.at[2])
     second_ref[y] = jnp.sum(first_ref[...], axis=0)
     for step in range(1, 16):
         to = (y + step) % 16
         send(second_ref.at[y], second_ref.at[y], send_sem.at[3], recv_sem.at[3], device_at(x, to))
     drain(second_ref.at[pl.ds(0, 15)], recv_sem.at[3])
-    third_ref[x] = jnp.sum(second_ref[...], axis=0)
-    for step in range(1, 8):
-        to = (x + step) % 8
-        send(third_ref.at[x], third_ref.at[x], send_sem.at[4], recv_sem.at[4], device_at(to, y))
-    drain(third_ref.at[pl.ds(0, 7)], recv_sem.at[4])
-    total = jnp.zeros((1, 1), F32)
-    for n in range(8):
-        pseudo = third_ref[n, 0:4, :]
-        model = model_ref[4 * n : 4 * n + 4, :]
-        pseudo_ref[4 * n : 4 * n + 4, :] = pseudo
-        rel_error = (pseudo - model) / model
-        total = total + jnp.sum(rel_error * rel_error, keepdims=True)
+    pseudo = jnp.sum(second_ref[...], axis=0)
+    pseudo_ref[...] = pseudo
+    model = model_ref[...]
+    rel_error = (pseudo - model) / model
+    total = jnp.sum(rel_error * rel_error, keepdims=True)
     misfit_ref[...] = total * (1.0 / LMAX)
     drain(mid_ref.at[pl.ds(0, 7)], send_sem.at[0])
     drain(land_ref.at[pl.ds(0, 15)], send_sem.at[1])
     drain(first_ref.at[pl.ds(0, 7)], send_sem.at[2])
     drain(second_ref.at[pl.ds(0, 15)], send_sem.at[3])
-    drain(third_ref.at[pl.ds(0, 7)], send_sem.at[4])
 
 
 VM = pl.BlockSpec(memory_space=pltpu.VMEM)
@@ -566,12 +560,11 @@
             pltpu.VMEM((32 * TILES, 128), F32),
             pltpu.VMEM((256, 128), F32),
             pltpu.VMEM((72, 128), F32),
-            pltpu.VMEM((8, 8, 128), F32),
-            pltpu.VMEM((8, 8, 128), F32),
-            pltpu.VMEM((16, 8, 128), F32),
-            pltpu.VMEM((8, 8, 128), F32),
-            dma((5,)),
-            dma((5,)),
+            pltpu.VMEM((32, 128), F32),
+            pltpu.VMEM((8, 32, 128), F32),
+            pltpu.VMEM((16, 32, 128), F32),
+            dma((4,)),
+            dma((4,)),
         ],
         compiler_params=pltpu.CompilerParams(
             collective_id=0, has_side_effects=True, vmem_limit_bytes=60 * 1024 * 1024

time: 45.6 us -> 41.3 us (0.906)
  Pallas kernels: 41.7 us -> 37.3 us
    pallas_call x1, Pallas kernels: 41.7 us -> 37.3 us  [on_device(): pl.pallas_call(everything, out_shape=(jax.ShapeDtypeStruct((32, 128), F32...]
where the time goes in v4:
time: 41.3 us; the launch traced here: 41 us
  Pallas kernels  37.3 us (90%)
  between operations  2.4 us (6%)
  local copies, waits for them, and re-layouts  1.32 us (3%)
    pallas_call x1, Pallas kernels, on_device(): pl.pallas_call(everything, out_shape=(jax.ShapeDtypeStruct((32, 128), F32...  37.3 us
    unnamed x1, local copies, waits for them, and re-layouts  1.32 us

profile of v4, /device:TPU:1, one launch (start us, length us, event | category | flops | bytes accessed | tf_op | source)
XLA Modules:
  0.0 41.0 jit_solution(442862000157691598)
XLA Ops:
  0.6 37.3 %shard_map.131 = (f32[32,128]{1,0:T(8,128)}, f32[1,1]{1,0:T(1,128)}) custom-call(f32[16,1024]{1,0:T(8,128)} %pixels_hbm.1, s32[1,16]{1,0:T(1,128)} %bitcast.7, s32[1,16]{1,0:T(1,128)} %bitcast.8, f32[32,128]{1,0:T(8,128)} %bitcast.5, f32[256]{0:T(256)} %constant.16.clone.logs_hbm, f32[128,64]{1,0:T(8,128)} %constant.17.clone.one_hbm, ...), custom_call_target="tpu_custom_call" | custom-call | tf_op jit(solution)/shard_map/pallas_call | solution.py:531
  38.0 1.3 %copy.16 = f32[4096]{0:T(1024)} copy(f32[4096]{0:T(1024)} %bitcast.6) | data formatting | bytes 32768

commit v5 on v4

--- a/solution.py
+++ b/solution.py
@@ -184,7 +184,7 @@
             degree = t + first
             down = t - order
             up = (degree + first + order).astype(F32)
-            weight = jnp.where(first + order == 0, 1.0, 2.0) * (1.0 / (CYCLES * CYCLE_PIX))
+            weight = jnp.where(first + order == 0, 1.0, 2.0)
             denom = jnp.maximum(down.astype(F32), 1.0) * jnp.maximum(up, 1.0) * both
             at = pl.ds(start + 8 * k, 8)
             coef_ref[at, :] = both * (2 * degree - 1).astype(F32)
@@ -369,11 +369,12 @@
         return carry
 
     def many(k, carry):
-        for n in range(3):
-            one(3 * k + n, carry)
+        for n in range(4):
+            one(4 * k + n, carry)
         return carry
 
-    lax.fori_loop(0, TILES // 3, many, 0)
+    lax.fori_loop(0, TILES // 4, many, 0)
+    one(TILES - 1, 0)
     row = lax.broadcasted_iota(jnp.int32, (256, 128), 0)
     column = lax.broadcasted_iota(jnp.int32, (256, 128), 1)
     quarters = jnp.where(row // 16 % 4 == column % 4, 1.0, 0.0).astype(BF16)
@@ -509,7 +510,7 @@
     pseudo = jnp.sum(second_ref[...], axis=0)
     pseudo_ref[...] = pseudo
     model = model_ref[...]
-    rel_error = (pseudo - model) / model
+    rel_error = (pseudo * (1.0 / (CYCLES * CYCLE_PIX)) - model) / model
     total = jnp.sum(rel_error * rel_error, keepdims=True)
     misfit_ref[...] = total * (1.0 / LMAX)
     drain(mid_ref.at[pl.ds(0, 7)], send_sem.at[0])
@@ -570,7 +571,7 @@
             collective_id=0, has_side_effects=True, vmem_limit_bytes=60 * 1024 * 1024
         ),
     )(pixels, block_ids.reshape(1, 16), block_mask.reshape(1, 16), model_cl.reshape(32, 128), half_logs(), *tables)
-    return pseudo_cl.reshape(LMAX), misfit.reshape(())
+    return pseudo_cl.reshape(LMAX) * (1.0 / (CYCLES * CYCLE_PIX)), misfit.reshape(())
 
 
 def solution(mesh):

time: 41.3 us -> 40.5 us (0.981)
  other arithmetic: 0 us -> 1.33 us
  local copies, waits for them, and re-layouts: 1.32 us -> 0 us
  Pallas kernels: 37.3 us -> 36.6 us
    mul x0 -> x1, other arithmetic: none -> 1.33 us  [on_device(): pseudo_cl.reshape(LMAX) * (1.0 / (CYCLES * CYCLE_PIX))]
    unnamed x1 -> x0, local copies, waits for them, and re-layouts: 1.32 us -> none
    pallas_call x1, Pallas kernels: 37.3 us -> 36.6 us  [on_device(): pl.pallas_call(everything, out_shape=(jax.ShapeDtypeStruct((32, 128), F32...]
where the time goes in v5:
time: 40.5 us; the launch traced here: 40.3 us
  Pallas kernels  36.6 us (90%)
  between operations  2.4 us (6%)
  other arithmetic  1.33 us (3%)
    pallas_call x1, Pallas kernels, on_device(): pl.pallas_call(everything, out_shape=(jax.ShapeDtypeStruct((32, 128), F32...  36.6 us
    mul x1, other arithmetic, on_device(): pseudo_cl.reshape(LMAX) * (1.0 / (CYCLES * CYCLE_PIX))  1.33 us

profile of v5, /device:TPU:1, one launch (start us, length us, event | category | flops | bytes accessed | tf_op | source)
XLA Modules:
  0.0 40.3 jit_solution(2942801808435736995)
XLA Ops:
  0.6 36.6 %shard_map.131 = (f32[32,128]{1,0:T(8,128)}, f32[1,1]{1,0:T(1,128)}) custom-call(f32[16,1024]{1,0:T(8,128)} %pixels_hbm.1, s32[1,16]{1,0:T(1,128)} %bitcast.7, s32[1,16]{1,0:T(1,128)} %bitcast.8, f32[32,128]{1,0:T(8,128)} %bitcast.6, f32[256]{0:T(256)} %constant.18.clone.logs_hbm, f32[128,64]{1,0:T(8,128)} %constant.19.clone.one_hbm, ...), custom_call_target="tpu_custom_call" | custom-call | tf_op jit(solution)/shard_map/pallas_call | solution.py:532
  37.2 1.3 %multiply_bitcast_fusion = f32[4096]{0:T(1024)} fusion(f32[32,128]{1,0:T(8,128)} %get-tuple-element.4), kind=kLoop, calls=%fused_computation | loop fusion | flops 4096 | bytes 32768 | tf_op jit(solution)/shard_map/mul | solution.py:574
